TPU v7x, 128 devices: a whole 4x4x4 slice. The times are simulated.
128 devices in a mesh: gx: 8 (over z, core), gy: 16 (over x, y).
Axes of the slice: x: 4, y: 4, z: 4, core: 2. Of those that a mesh axis runs over, the one named last changes fastest.
Arguments:
- leaf_front: float32 [12288, 24576], P('gx', 'gy'), may hold values from -18 to 18, as said below
- place_pairs: int32 [8, 128], P('gx', 'gy'), may hold values from 0 to 11, as said below
- place_quads: int32 [8, 128], P('gx', 'gy'), may hold values from 0 to 11, as said below
Outputs:
- pair_panel: float32 [12288, 8192], P('gx', 'gy')
- quad_panel: float32 [12288, 8192], P('gx', 'gy')
- quad_update: float32 [8192, 16384], P('gx', 'gy')
Inputs may be any that keep to these rules, and one draw needn't show every extreme that they name: `leaf_front`: each tile is symmetric positive definite. `place_pairs`: each device's 8 entries are distinct; the two devices (q, j) and (q + 4, j) both name blocks 0 to 3, and each names 4 of the other blocks that the other does not name. `place_quads`: devices (q, j) and (q + 4, j) hold equal rows; each row's 8 entries are distinct; the rows of (q, r) and (q, r + 8) both name blocks 0 to 3, and each names 4 of the other blocks that the other does not name.
All inputs are finite; a program needn't handle non-finite values.
Results may differ from a plain program's by a relative error of at most 0.0003.
Values sent between devices are 32-bit elements; how exact they have to be, the bound alone decides.
A program may use at most 192 MiB of HBM per device.

v0:
```python
import jax
import jax.numpy as jnp
from jax import lax
from jax.sharding import PartitionSpec as P

NI = 512
NS = 512


def shifted(shard, axis, by):
    size = lax.axis_size(axis)
    return lax.ppermute(shard, axis, [(i, (i + by) % size) for i in range(size)])


def leaf_update(front_tile):
    interior = jnp.linalg.cholesky(front_tile[:NI, :NI])
    coupled = jax.scipy.linalg.solve_triangular(interior, front_tile[:NI, NI:], lower=True)
    return front_tile[NI:, NI:] - jnp.dot(coupled.T, coupled, precision=lax.Precision.HIGHEST)


def extend_add(update, placement):
    blocks_count = placement.shape[0]
    block_size = update.shape[0] // blocks_count
    joined_blocks = blocks_count + blocks_count // 2
    onehot = (placement[None, :] == jnp.arange(joined_blocks, dtype=jnp.int32)[:, None]).astype(
        jnp.float32
    )
    blocks = update.reshape(blocks_count, block_size, blocks_count, block_size)
    spread = jnp.einsum("ja,aibk,lb->jilk", onehot, blocks, onehot, precision=lax.Precision.HIGHEST)
    return spread.reshape(joined_blocks * block_size, joined_blocks * block_size)


def partial_factor(joined):
    corner = jnp.linalg.cholesky(joined[:NS, :NS])
    coupled = jax.scipy.linalg.solve_triangular(corner, joined[:NS, NS:], lower=True)
    factor_panel = jnp.concatenate([corner, coupled.T], axis=0)
    update = joined[NS:, NS:] - jnp.dot(coupled.T, coupled, precision=lax.Precision.HIGHEST)
    return (factor_panel, update)


def shards(leaf_front, place_pairs, place_quads):
    update_leaf = leaf_update(leaf_front)
    pair_row = place_pairs[0]
    quad_row = place_quads[0]
    half_cols = lax.axis_size("gx") // 2
    half_rows = lax.axis_size("gy") // 2
    other_update, other_place = shifted(
        (update_leaf, pair_row.astype(jnp.float32)), "gx", half_cols
    )
    joined_pair = extend_add(update_leaf, pair_row) + extend_add(
        other_update, other_place.astype(jnp.int32)
    )
    pair_panel, update_pair = partial_factor(joined_pair)
    partner_update, partner_place = shifted(
        (update_pair, quad_row.astype(jnp.float32)), "gy", half_rows
    )
    joined_quad = extend_add(update_pair, quad_row) + extend_add(
        partner_update, partner_place.astype(jnp.int32)
    )
    quad_panel, quad_update = partial_factor(joined_quad)
    return (pair_panel, quad_panel, quad_update)


def solution(mesh):
    in_specs = (P("gx", "gy"), P("gx", "gy"), P("gx", "gy"))
    out_specs = (P("gx", "gy"), P("gx", "gy"), P("gx", "gy"))
    return jax.shard_map(shards, mesh=mesh, in_specs=in_specs, out_specs=out_specs, check_vma=False)
```

profile of v0, /device:TPU:0, one launch (start us, length us, event | category | flops | bytes accessed | tf_op | source)
XLA Modules:
  0.0 774.2 jit_solution(7639634194127469906)
XLA Ops:
  3.7 11.7 %cholesky.374 = f32[128,128]{1,0:T(8,128)S(1)} custom-call(f32[128,128]{1,0:T(8,128)S(1)} %cholesky.586), custom_call_target="Cholesky" | custom-call | tf_op jit(solution)/shard_map/jit(cholesky)/cholesky | solution.py:16
  26.1 11.7 %cholesky.393 = f32[128,128]{1,0:T(8,128)S(1)} custom-call(f32[128,128]{1,0:T(8,128)S(1)} %cholesky.590), custom_call_target="Cholesky" | custom-call | tf_op jit(solution)/shard_map/jit(cholesky)/cholesky | solution.py:16
  37.9 10.0 %custom-call.32 = f32[1,128,128]{1,2,0:T(8,128)S(1)} custom-call(f32[1,128,128]{2,1,0:T(8,128)S(1)} %get-tuple-element.94), custom_call_target="InvertDiagBlocksLowerTriangular" | custom-call | tf_op jit(solution)/shard_map/jit(cholesky)/cholesky | solution.py:16
  48.5 11.7 %cholesky.414 = f32[128,128]{1,0:T(8,128)S(1)} custom-call(f32[128,128]{1,0:T(8,128)S(1)} %cholesky.595), custom_call_target="Cholesky" | custom-call | tf_op jit(solution)/shard_map/jit(cholesky)/cholesky | solution.py:16
  70.7 11.7 %cholesky.431 = f32[128,128]{1,0:T(8,128)S(1)} custom-call(f32[128,128]{1,0:T(8,128)S(1)} %convolution_subtract_fusion.14), custom_call_target="Cholesky" | custom-call | tf_op jit(solution)/shard_map/jit(cholesky)/cholesky | solution.py:16
  95.6 39.3 %custom-call.34 = f32[4,128,128]{1,2,0:T(8,128)S(1)} custom-call(f32[4,128,128]{2,1,0:T(8,128)S(1)} %get-tuple-element.25), custom_call_target="InvertDiagBlocksLowerTriangular" | custom-call | tf_op jit(solution)/shard_map/jit(_solve_triangular)/triangular_solve | solution.py:17
  174.1 74.8 %collective-permute-done.1 = f32[8]{0:T(128)S(1)} collective-permute-done((f32[8]{0:T(128)S(1)}, f32[8]{0:T(128)S(1)}, u32[]{:S(2)}, u32[]{:S(2)}) %collective-permute-start.1) | collective-permute-done | bytes 64 | tf_op jit(solution)/shard_map/ppermute | solution.py:12
  259.0 13.2 %add_bitcast_fusion.1 = f32[12,128,12,128]{3,2,0,1:T(8,128)} fusion(f32[128,128,12,12]{1,3,2,0:T(8,128)S(1)} %fusion.6, f32[128,8,128,12]{2,3,1,0:T(8,128)} %fusion.16, s32[8]{0:T(128)S(1)} %convert_element_type.17), kind=kOutput, calls=%fused_computation.7 | convolution fusion | flops 228851808 | bytes 25165856 | tf_op jit(solution)/shard_map/ja,aibk,lb->jilk/dot_general | solution.py:29
  272.2 10.3 %copy.21 = f32[12,128,12,128]{3,2,1,0:T(8,128)} copy(f32[12,128,12,128]{3,2,0,1:T(8,128)} %add_bitcast_fusion.1) | data formatting | bytes 18874368 | tf_op jit(solution)/shard_map/add | solution.py:50
  297.3 11.7 %cholesky.446 = f32[128,128]{1,0:T(8,128)S(1)} custom-call(f32[128,128]{1,0:T(8,128)S(1)} %cholesky.599), custom_call_target="Cholesky" | custom-call | tf_op jit(solution)/shard_map/jit(cholesky)/cholesky | solution.py:34
  319.8 11.7 %cholesky.465 = f32[128,128]{1,0:T(8,128)S(1)} custom-call(f32[128,128]{1,0:T(8,128)S(1)} %cholesky.603), custom_call_target="Cholesky" | custom-call | tf_op jit(solution)/shard_map/jit(cholesky)/cholesky | solution.py:34
  342.1 11.7 %cholesky.486 = f32[128,128]{1,0:T(8,128)S(1)} custom-call(f32[128,128]{1,0:T(8,128)S(1)} %cholesky.608), custom_call_target="Cholesky" | custom-call | tf_op jit(solution)/shard_map/jit(cholesky)/cholesky | solution.py:34
  353.8 10.0 %custom-call.37 = f32[1,128,128]{1,2,0:T(8,128)S(1)} custom-call(f32[1,128,128]{2,1,0:T(8,128)S(1)} %get-tuple-element.81), custom_call_target="InvertDiagBlocksLowerTriangular" | custom-call | tf_op jit(solution)/shard_map/jit(cholesky)/cholesky | solution.py:34
  364.4 11.7 %cholesky.503 = f32[128,128]{1,0:T(8,128)S(1)} custom-call(f32[128,128]{1,0:T(8,128)S(1)} %convolution_subtract_fusion.13), custom_call_target="Cholesky" | custom-call | tf_op jit(solution)/shard_map/jit(cholesky)/cholesky | solution.py:34
  389.7 39.7 %custom-call.38 = f32[4,128,128]{1,2,0:T(8,128)S(1)} custom-call(f32[4,128,128]{2,1,0:T(8,128)S(1)} %get-tuple-element.26), custom_call_target="InvertDiagBlocksLowerTriangular" | custom-call | tf_op jit(solution)/shard_map/jit(_solve_triangular)/triangular_solve | solution.py:35
  452.1 90.0 %collective-permute-done.3 = f32[8]{0:T(128)S(1)} collective-permute-done((f32[8]{0:T(128)S(1)}, f32[8]{0:T(128)S(1)}, u32[]{:S(2)}, u32[]{:S(2)}) %collective-permute-start.3) | collective-permute-done | bytes 64 | tf_op jit(solution)/shard_map/ppermute | solution.py:12
  573.4 13.2 %add_bitcast_fusion = f32[12,128,12,128]{3,2,0,1:T(8,128)} fusion(f32[128,128,12,12]{1,3,2,0:T(8,128)S(1)} %fusion.2, f32[128,8,128,12]{2,3,1,0:T(8,128)} %fusion.12, s32[8]{0:T(128)S(1)} %convert_element_type.19), kind=kOutput, calls=%fused_computation.6 | convolution fusion | flops 228851808 | bytes 25165856 | tf_op jit(solution)/shard_map/ja,aibk,lb->jilk/dot_general | solution.py:29
  586.6 10.3 %copy.25 = f32[12,128,12,128]{3,2,1,0:T(8,128)} copy(f32[12,128,12,128]{3,2,0,1:T(8,128)} %add_bitcast_fusion) | data formatting | bytes 18874368 | tf_op jit(solution)/shard_map/add | solution.py:57
  611.7 11.7 %cholesky.518 = f32[128,128]{1,0:T(8,128)S(1)} custom-call(f32[128,128]{1,0:T(8,128)S(1)} %cholesky.612), custom_call_target="Cholesky" | custom-call | tf_op jit(solution)/shard_map/jit(cholesky)/cholesky | solution.py:34
  634.3 11.7 %cholesky.537 = f32[128,128]{1,0:T(8,128)S(1)} custom-call(f32[128,128]{1,0:T(8,128)S(1)} %cholesky.616), custom_call_target="Cholesky" | custom-call | tf_op jit(solution)/shard_map/jit(cholesky)/cholesky | solution.py:34
  656.5 11.7 %cholesky.558 = f32[128,128]{1,0:T(8,128)S(1)} custom-call(f32[128,128]{1,0:T(8,128)S(1)} %cholesky.621), custom_call_target="Cholesky" | custom-call | tf_op jit(solution)/shard_map/jit(cholesky)/cholesky | solution.py:34
  678.9 11.7 %cholesky.575 = f32[128,128]{1,0:T(8,128)S(1)} custom-call(f32[128,128]{1,0:T(8,128)S(1)} %convolution_subtract_fusion.12), custom_call_target="Cholesky" | custom-call | tf_op jit(solution)/shard_map/jit(cholesky)/cholesky | solution.py:34
  697.1 11.7 %while.8 = (s32[]{:T(128)}, f32[512,512]{1,0:T(8,128)}, s32[4,2]{0,1:T(2,128)S(1)}, f32[4,128,128]{2,1,0:T(8,128)S(1)}, s32[]{:T(128)}) while((s32[]{:T(128)}, f32[512,512]{1,0:T(8,128)}, s32[4,2]{0,1:T(2,128)S(1)}, f32[4,128,128]{2,1,0:T(8,128)S(1)}, s32[]{:T(128)}) %tuple.90), condition=%wide.while_cond.clone.1, body=%wide.while_body.clone.1.sunk | while | flops 2 | bytes 131189 | solution.py:35
  708.8 39.6 %custom-call.42 = f32[4,128,128]{1,2,0:T(8,128)S(1)} custom-call(f32[4,128,128]{2,1,0:T(8,128)S(1)} %get-tuple-element.27), custom_call_target="InvertDiagBlocksLowerTriangular" | custom-call | tf_op jit(solution)/shard_map/jit(_solve_triangular)/triangular_solve | solution.py:35
  (188 shorter events, 289.4 us)
Async XLA Ops:
  144.0 13.9 %copy-start.4 = (s32[1,8]{1,0:T(1,128)S(1)}, s32[1,8]{1,0:T(1,128)}, u32[]{:S(2)}) copy-start(s32[1,8]{1,0:T(1,128)} %param.7) | copy-start | bytes 100
  154.0 94.9 %collective-permute-start = (f32[1024,1024]{1,0:T(8,128)}, f32[1024,1024]{1,0:T(8,128)}, u32[]{:S(2)}, u32[]{:S(2)}) collective-permute-start(f32[1024,1024]{1,0:T(8,128)} %slice_subtract_fusion.2), channel_id=1, source_target_pairs={{0,64},{16,80},{32,96},{48,112},{64,0},{80,16},{96,32},{112,48},{1... | collective-permute-start | bytes 12582920 | tf_op jit(solution)/shard_map/ppermute | solution.py:12
  158.0 90.9 %collective-permute-start.1 = (f32[8]{0:T(128)S(1)}, f32[8]{0:T(128)S(1)}, u32[]{:S(2)}, u32[]{:S(2)}) collective-permute-start(f32[8]{0:T(128)S(1)} %bitcast_convert_fusion.1), channel_id=1, source_target_pairs={{0,64},{16,80},{32,96},{48,112},{64,0},{80,16},{96,32},{112,48},{1... | collective-permute-start | bytes 104 | tf_op jit(solution)/shard_map/ppermute | solution.py:12
  291.8 3.6 copy-start.1
  389.7 43.7 %copy-start.3 = (f32[512,512]{1,0:T(8,128)}, f32[512,512]{1,0:T(8,128)S(1)}, u32[]{:S(2)}) copy-start(f32[512,512]{1,0:T(8,128)S(1)} %get-tuple-element.240) | copy-start | bytes 3145732
  438.7 12.9 %copy-start.5 = (s32[1,8]{1,0:T(1,128)S(1)}, s32[1,8]{1,0:T(1,128)}, u32[]{:S(2)}) copy-start(s32[1,8]{1,0:T(1,128)} %param.8) | copy-start | bytes 100
  448.6 114.7 %collective-permute-start.2 = (f32[1024,1024]{1,0:T(8,128)}, f32[1024,1024]{1,0:T(8,128)}, u32[]{:S(2)}, u32[]{:S(2)}) collective-permute-start(f32[1024,1024]{1,0:T(8,128)} %slice_subtract_fusion.1), channel_id=1, source_target_pairs={{0,8},{1,9},{2,10},{3,11},{4,12},{5,13},{6,14},{7,15},{8,0},{9,1},... | collective-permute-start | bytes 12582920 | tf_op jit(solution)/shard_map/ppermute | solution.py:12
  451.6 90.5 %collective-permute-start.3 = (f32[8]{0:T(128)S(1)}, f32[8]{0:T(128)S(1)}, u32[]{:S(2)}, u32[]{:S(2)}) collective-permute-start(f32[8]{0:T(128)S(1)} %bitcast_convert_fusion), channel_id=1, source_target_pairs={{0,8},{1,9},{2,10},{3,11},{4,12},{5,13},{6,14},{7,15},{8,0},{9,1},... | collective-permute-start | bytes 104 | tf_op jit(solution)/shard_map/ppermute | solution.py:12
  543.5 1.2 copy-start.2
  606.2 3.6 copy-start
  655.8 103.8 %slice-start = ((s8[9437184]{0:T(1024)(128)(4,1)}), s8[1048576]{0:T(1024)(128)(4,1)S(1)}, s32[]{:S(2)}) async-start(s8[9437184]{0:T(1024)(128)(4,1)} %bitcast.210), calls=%async_computation | async-start | bytes 2097152
  748.4 11.3 %slice-start.1 = ((s8[9437184]{0:T(1024)(128)(4,1)}), s8[4194304]{0:T(1024)(128)(4,1)S(1)}, s32[]{:S(2)}) async-start(s8[9437184]{0:T(1024)(128)(4,1)} %bitcast.210), calls=%async_computation.1 | async-start | bytes 8388608
  755.0 4.6 slice-start.2
where the time goes:
time: 784 us; the launch traced here: 774 us
  other arithmetic  366 us (47%)
  waiting for transfers between devices  165 us (21%)
  matrix products  127 us (16%)
  local copies, waits for them, and re-layouts  98.2 us (13%)
  between operations  9.6 us (1%)
    ppermute x4, waiting for transfers between devices, shifted(): lax.ppermute(shard, axis, [(i, (i + by) % size) for i in range(size)])  165 us
    another operation x30, other arithmetic, partial_factor(): corner = jnp.linalg.cholesky(joined[:NS, :NS])  159 us
    another operation x4, other arithmetic, partial_factor(): jax.scipy.linalg.solve_triangular(corner, joined[:NS, NS:], lower=True)  80.8 us
    another operation x14, other arithmetic, leaf_update(): interior = jnp.linalg.cholesky(front_tile[:NI, :NI])  78.6 us
    dot_general x8, matrix products, extend_add(): jnp.einsum('ja,aibk,lb->jilk', onehot, blocks, onehot, precision=lax.Prec...  65.4 us
    unnamed x29, local copies, waits for them, and re-layouts  45.6 us
    another operation x3, other arithmetic, leaf_update(): jax.scipy.linalg.solve_triangular(interior, front_tile[:NI, NI:], lower=T...  39.8 us
    another operation x24, local copies, waits for them, and re-layouts, partial_factor(): jax.scipy.linalg.solve_triangular(corner, joined[:NS, NS:], lower=True)  19.5 us
  transfers between devices with their start and end apart: 4, of which 2 were waited for; matrix products, arithmetic and copies ran while one was open for 5% of the time, Pallas kernels for 0%

commit v1 on v0

v1 whole, which is shorter than its diff:
```python
import functools

import jax
import jax.numpy as jnp
from jax import lax
from jax.experimental import pallas as pl
from jax.experimental.pallas import tpu as pltpu
from jax.sharding import PartitionSpec as P

F32 = jnp.float32
BF16 = jnp.bfloat16
B = 128
NS = 512
NB = 1024
NJ = 1536
LOWER = [(a, b) for a in range(4) for b in range(a + 1)]
VMEM = pl.BlockSpec(memory_space=pltpu.VMEM)
SMEM = pl.BlockSpec(memory_space=pltpu.SMEM)
ANY = pl.BlockSpec(memory_space=pl.ANY)


def full(x):
    return jnp.broadcast_to(x, (8, B))


def split(x):
    hi = x.astype(BF16)
    return hi, (x - hi.astype(F32)).astype(BF16)


def dot3(a, b, dims):
    def one(x, y):
        return lax.dot_general(x, y, (dims, ((), ())), preferred_element_type=F32)

    return (one(a[1], b[0]) + one(a[0], b[1])) + one(a[0], b[0])


NN = ((1,), (0,))
NT = ((1,), (1,))


def factor_block(m):
    for p in range(B // 8):
        r = 8 * p
        x0, x1 = m[r : r + 8, 0:B], m[r : r + 8, B : 2 * B]
        xs = [full(x0[i : i + 1, :]) for i in range(8)]
        ys = [full(x1[i : i + 1, :]) for i in range(8)]
        col = [full(x0[:, r + j : r + j + 1]) for j in range(8)]
        e = [[full(col[j][i : i + 1, :]) if j >= i else None for j in range(8)] for i in range(8)]
        inv = [None] * 8
        for k in range(8):
            inv[k] = lax.rsqrt(e[k][k])
            for j in range(k + 1, 8):
                e[k][j] = e[k][j] * inv[k]
            xs[k], ys[k] = xs[k] * inv[k], ys[k] * inv[k]
            for i in range(k + 1, 8):
                for j in range(i, 8):
                    e[i][j] = e[i][j] - e[k][i] * e[k][j]
                xs[i] = xs[i] - e[k][i] * xs[k]
                ys[i] = ys[i] - e[k][i] * ys[k]
        for k in range(8):
            m[r + k : r + k + 1, 0:B] = xs[k][0:1, :]
            m[r + k : r + k + 1, B : 2 * B] = ys[k][0:1, :]
        for q in range(p + 1, B // 8):
            s = 8 * q
            y0, y1 = m[s : s + 8, 0:B], m[s : s + 8, B : 2 * B]
            c = [full(y0[:, r + j : r + j + 1]) for j in range(8)]
            for k in range(8):
                c[k] = c[k] * inv[k]
                for j in range(k + 1, 8):
                    c[j] = c[j] - c[k] * e[k][j]
                y0 = y0 - c[k] * xs[k]
                y1 = y1 - c[k] * ys[k]
            m[s : s + 8, 0:B] = y0
            m[s : s + 8, B : 2 * B] = y1


def eye_block():
    i0 = lax.broadcasted_iota(jnp.int32, (B, B), 0)
    i1 = lax.broadcasted_iota(jnp.int32, (B, B), 1)
    return i0, i1, jnp.where(i0 == i1, 1.0, 0.0).astype(F32)


def factor_front(g, m, l_ref):
    i0, i1, eye = eye_block()
    m[:, 0:B] = g[0:B, 0:B]
    m[:, B : 2 * B] = eye
    l_ref[...] = jnp.zeros((NS, NS), F32)

    def step(k, carry):
        factor_block(m)
        for kk in range(4):

            @pl.when(k == kk)
            def _(kk=kk):
                c, n = B * kk, B * (kk + 1)
                inverse = m[:, B : 2 * B]
                l_ref[c:n, c:n] = jnp.where(i0 <= i1, m[:, 0:B], 0.0).T
                g[c:n, NS + c : NS + n] = inverse
                inv2 = split(inverse)
                if kk > 0:
                    g[c:n, NS : NS + c] = dot3(inv2, split(g[c:n, NS : NS + c]), NN)
                if kk < 3:
                    right = dot3(inv2, split(g[c:n, n:NS]), NN)
                    below = right.T
                    l_ref[n:NS, c:n] = below
                    below2 = split(below)
                    g[n:NS, n:NS] = g[n:NS, n:NS] - dot3(below2, split(right), NN)
                    m[:, 0:B] = g[n : n + B, n : n + B]
                    m[:, B : 2 * B] = eye
                    g[n:NS, NS : NS + n] = g[n:NS, NS : NS + n] - dot3(below2, split(g[c:n, NS : NS + n]), NN)

        return carry

    lax.fori_loop(0, 4, step, 0)


def solve_rows(bt, g, vt, store):
    inv2 = split(g)
    for h in range(4):
        rows = dot3(split(bt[256 * h : 256 * (h + 1), :]), inv2, NT)
        vt[256 * h : 256 * (h + 1), :] = rows
        store(2 * h, rows[0:B])
        store(2 * h + 1, rows[B : 2 * B])


def order_of(place):
    rank = [sum((place[j] < place[i]).astype(jnp.int32) for j in range(8) if j != i) for i in range(8)]
    return [sum(jnp.where(rank[i] == a, i, 0) for i in range(8)) for a in range(8)]


def source_of(place):
    named, before, result = [], 0, []
    for u in range(8):
        mine = sum((place[i] == 4 + u).astype(jnp.int32) for i in range(8))
        result.append(jnp.where(mine == 1, before, 4 + u - before))
        before = before + mine
    return result


def leaf_solve_kernel(place_ref, leaf, vt, ss, g, m, bt, base, l_buf, sems):
    order = order_of([place_ref[0, i] for i in range(8)])
    at = [pl.multiple_of(NS + B * order[a], B) for a in range(8)]
    first = pltpu.make_async_copy(leaf.at[0:NS, 0:NS], g.at[:, 0:NS], sems.at[0])
    first.start()
    copies = [pltpu.make_async_copy(leaf.at[pl.ds(at[a], B), 0:NS], bt.at[B * a : B * a + B], sems.at[1 + a]) for a in range(8)]
    copies += [
        pltpu.make_async_copy(leaf.at[pl.ds(at[a], B), pl.ds(at[b], B)], base.at[t], sems.at[9 + t])
        for t, (a, b) in enumerate(LOWER)
    ]
    for copy in copies:
        copy.start()
    g[:, NS:NB] = jnp.zeros((NS, NS), F32)
    first.wait()
    factor_front(g, m, l_buf)
    for copy in copies:
        copy.wait()
    solve_rows(bt, g[:, NS:NB], vt, lambda i, rows: None)
    sep_update(vt, ss, lambda t: base[t])


def sep_update(vt, out, base):
    v2 = split(vt[0:NS, :])
    for h in range(2):
        rows = slice(256 * h, 256 * (h + 1))
        prod = dot3((v2[0][rows], v2[1][rows]), (v2[0][0 : 256 * (h + 1)], v2[1][0 : 256 * (h + 1)]), NT)
        for t, (a, b) in enumerate(LOWER):
            if a // 2 == h:
                out[t] = base(t) - prod[B * (a % 2) : B * (a % 2) + B, B * b : B * b + B]


def rest_update(vt, rs, rr, rs_base, rr_base):
    v2 = split(vt[...])
    for h in range(2):
        rows = slice(NS + 256 * h, NS + 256 * (h + 1))
        last = NS + 256 * (h + 1)
        prod = dot3((v2[0][rows], v2[1][rows]), (v2[0][0:last], v2[1][0:last]), NT)
        for a in (2 * h, 2 * h + 1):
            r = B * (a % 2)
            for b in range(4):
                rs[B * a : B * a + B, B * b : B * b + B] = rs_base(a, b) - prod[r : r + B, B * b : B * b + B]
        for t, (a, b) in enumerate(LOWER):
            if a // 2 == h:
                rr[t] = rr_base(t) - prod[B * (a % 2) : B * (a % 2) + B, NS + B * b : NS + B * b + B]


def leaf_rest_kernel(place_ref, leaf, vt, rs, rr, rs_buf, rr_buf, sems):
    order = order_of([place_ref[0, i] for i in range(8)])
    at = [pl.multiple_of(NS + B * order[a], B) for a in range(8)]
    copies = [
        pltpu.make_async_copy(leaf.at[pl.ds(at[4 + a], B), pl.ds(at[b], B)], rs_buf.at[4 * a + b], sems.at[4 * a + b])
        for a in range(4)
        for b in range(4)
    ]
    copies += [
        pltpu.make_async_copy(leaf.at[pl.ds(at[4 + a], B), pl.ds(at[4 + b], B)], rr_buf.at[t], sems.at[16 + t])
        for t, (a, b) in enumerate(LOWER)
    ]
    for copy in copies:
        copy.start()
    for copy in copies:
        copy.wait()
    rest_update(vt, rs, rr, lambda a, b: rs_buf[4 * a + b], lambda t: rr_buf[t])


def leaf_stage(leaf, place):
    vt, ss = pl.pallas_call(
        leaf_solve_kernel,
        out_shape=(jax.ShapeDtypeStruct((NB, NS), F32), jax.ShapeDtypeStruct((10, B, B), F32)),
        in_specs=[SMEM, ANY],
        out_specs=(VMEM, VMEM),
        scratch_shapes=[
            pltpu.VMEM((NS, NB), F32),
            pltpu.VMEM((B, 2 * B), F32),
            pltpu.VMEM((NB, NS), F32),
            pltpu.VMEM((10, B, B), F32),
            pltpu.VMEM((NS, NS), F32),
            pltpu.SemaphoreType.DMA((19,)),
        ],
        cost_estimate=pl.CostEstimate(flops=10**10, bytes_accessed=10**7, transcendentals=0),
        name="leaf_solve",
    )(place, leaf)

    def rest():
        return pl.pallas_call(
            leaf_rest_kernel,
            out_shape=(jax.ShapeDtypeStruct((NS, NS), F32), jax.ShapeDtypeStruct((10, B, B), F32)),
            in_specs=[SMEM, ANY, VMEM],
            out_specs=(VMEM, VMEM),
            scratch_shapes=[pltpu.VMEM((16, B, B), F32), pltpu.VMEM((10, B, B), F32), pltpu.SemaphoreType.DMA((26,))],
            cost_estimate=pl.CostEstimate(flops=3 * 10**9, bytes_accessed=10**7, transcendentals=0),
            name="leaf_rest",
        )(place, leaf, vt)

    return ss, rest


def factor_kernel(own, other, l_ref, inverse, g, m):
    for t, (a, b) in enumerate(LOWER):
        block = own[t] + other[t]
        g[B * a : B * a + B, B * b : B * b + B] = block
        if a != b:
            g[B * b : B * b + B, B * a : B * a + B] = block.T
    g[:, NS:NB] = jnp.zeros((NS, NS), F32)
    factor_front(g, m, l_ref)
    inverse[...] = g[:, NS:NB]


def factor_stage(own, other):
    return pl.pallas_call(
        factor_kernel,
        out_shape=(jax.ShapeDtypeStruct((NS, NS), F32), jax.ShapeDtypeStruct((NS, NS), F32)),
        in_specs=[VMEM, VMEM],
        out_specs=(VMEM, VMEM),
        scratch_shapes=[pltpu.VMEM((NS, NB), F32), pltpu.VMEM((B, 2 * B), F32)],
        cost_estimate=pl.CostEstimate(flops=10**10, bytes_accessed=4 * 10**6, transcendentals=0),
        name="factor",
    )(own, other)


def gather_rows(rs_own, rs_other, source, bt):
    for a in range(8):

        @pl.when(source[a] < 4)
        def _(a=a):
            bt[B * a : B * a + B, :] = rs_own[pl.ds(pl.multiple_of(B * source[a], B), B), :]

        @pl.when(source[a] >= 4)
        def _(a=a):
            bt[B * a : B * a + B, :] = rs_other[pl.ds(pl.multiple_of(B * (source[a] - 4), B), B), :]


def spread_rest(rr_own, rr_other, blocks):
    for h, rr in enumerate((rr_own, rr_other)):
        for t, (a, b) in enumerate(LOWER):
            block = rr[t]
            blocks[16 * h + 4 * a + b] = block
            if a != b:
                blocks[16 * h + 4 * b + a] = block.T
    blocks[32] = jnp.zeros((B, B), F32)


def block_at(source, a, b):
    sa, sb = source[a], source[b]
    same = (sa < 4) == (sb < 4)
    return jnp.where(same, jnp.where(sa < 4, 0, 16) + 4 * (sa % 4) + sb % 4, 32)


def pair_solve_kernel(pair_ref, quad_ref, l_ref, inverse, rs_own, rs_other, rr_own, rr_other, panel, vt, ss, blocks, bt):
    order = order_of([quad_ref[0, i] for i in range(8)])
    where = source_of([pair_ref[0, i] for i in range(8)])
    source = [sum(jnp.where(order[a] == u, where[u], 0) for u in range(8)) for a in range(8)]
    gather_rows(rs_own, rs_other, source, bt)
    panel[0:NS, :] = l_ref[...]

    def store(i, rows):
        panel[pl.ds(pl.multiple_of(NS + B * order[i], B), B), :] = rows

    solve_rows(bt, inverse[...], vt, store)
    spread_rest(rr_own, rr_other, blocks)
    sep_update(vt, ss, lambda t: blocks[block_at(source, *LOWER[t])])


def pair_rest_kernel(pair_ref, quad_ref, vt, rr_own, rr_other, rs, rr, blocks):
    order = order_of([quad_ref[0, i] for i in range(8)])
    where = source_of([pair_ref[0, i] for i in range(8)])
    source = [sum(jnp.where(order[a] == u, where[u], 0) for u in range(8)) for a in range(8)]
    spread_rest(rr_own, rr_other, blocks)
    rest_update(
        vt,
        rs,
        rr,
        lambda a, b: blocks[block_at(source, 4 + a, b)],
        lambda t: blocks[block_at(source, 4 + LOWER[t][0], 4 + LOWER[t][1])],
    )


def pair_stage(pair, quad, l_full, inverse, rs_own, rs_other, rr_own, rr_other):
    panel, vt, ss = pl.pallas_call(
        pair_solve_kernel,
        out_shape=(
            jax.ShapeDtypeStruct((NJ, NS), F32),
            jax.ShapeDtypeStruct((NB, NS), F32),
            jax.ShapeDtypeStruct((10, B, B), F32),
        ),
        in_specs=[SMEM, SMEM] + [VMEM] * 6,
        out_specs=(VMEM,) * 3,
        scratch_shapes=[pltpu.VMEM((33, B, B), F32), pltpu.VMEM((NB, NS), F32)],
        cost_estimate=pl.CostEstimate(flops=3 * 10**9, bytes_accessed=10**7, transcendentals=0),
        name="pair_solve",
    )(pair, quad, l_full, inverse, rs_own, rs_other, rr_own, rr_other)

    def rest():
        return pl.pallas_call(
            pair_rest_kernel,
            out_shape=(jax.ShapeDtypeStruct((NS, NS), F32), jax.ShapeDtypeStruct((10, B, B), F32)),
            in_specs=[SMEM, SMEM] + [VMEM] * 3,
            out_specs=(VMEM, VMEM),
            scratch_shapes=[pltpu.VMEM((33, B, B), F32)],
            cost_estimate=pl.CostEstimate(flops=3 * 10**9, bytes_accessed=10**7, transcendentals=0),
            name="pair_rest",
        )(pair, quad, vt, rr_own, rr_other)

    return panel, ss, rest


def quad_kernel(quad_ref, l_ref, inverse, rs_own, rs_other, rr_own, rr_other, panel, update, blocks, bt, vt):
    source = source_of([quad_ref[0, i] for i in range(8)])
    gather_rows(rs_own, rs_other, source, bt)
    panel[0:NS, :] = l_ref[...]

    def store(i, rows):
        panel[NS + B * i : NS + B * i + B, :] = rows

    solve_rows(bt, inverse[...], vt, store)
    spread_rest(rr_own, rr_other, blocks)
    v2 = split(vt[...])
    for h in range(4):
        rows = slice(256 * h, 256 * (h + 1))
        last = 256 * (h + 1)
        prod = dot3((v2[0][rows], v2[1][rows]), (v2[0][0:last], v2[1][0:last]), NT)
        for a in (2 * h, 2 * h + 1):
            r = B * (a % 2)
            for b in range(a + 1):
                block = blocks[block_at(source, a, b)] - prod[r : r + B, B * b : B * b + B]
                update[B * a : B * a + B, B * b : B * b + B] = block
                if a != b:
                    update[B * b : B * b + B, B * a : B * a + B] = block.T


def quad_stage(quad, l_full, inverse, rs_own, rs_other, rr_own, rr_other):
    return pl.pallas_call(
        quad_kernel,
        out_shape=(jax.ShapeDtypeStruct((NJ, NS), F32), jax.ShapeDtypeStruct((NB, NB), F32)),
        in_specs=[SMEM] + [VMEM] * 6,
        out_specs=(VMEM, VMEM),
        scratch_shapes=[pltpu.VMEM((33, B, B), F32), pltpu.VMEM((NB, NS), F32), pltpu.VMEM((NB, NS), F32)],
        cost_estimate=pl.CostEstimate(flops=4 * 10**9, bytes_accessed=10**7, transcendentals=0),
        name="quad",
    )(quad, l_full, inverse, rs_own, rs_other, rr_own, rr_other)


def swapped(value, axis):
    size = lax.axis_size(axis)
    return lax.ppermute(value, axis, [(i, (i + size // 2) % size) for i in range(size)])


def exchange(ss, rest, axis):
    other_ss = swapped(ss, axis)
    rs, rr = rest()
    other_ss, rs_late, rr_late = lax.optimization_barrier((other_ss, rs, rr))
    return other_ss, rs, rr, swapped(rs_late, axis), swapped(rr_late, axis)


def shards(leaf_front, place_pairs, place_quads):
    ss, rest = leaf_stage(leaf_front, place_pairs)
    other_ss, rs, rr, other_rs, other_rr = exchange(ss, rest, "gx")
    l_pair, inverse = factor_stage(ss, other_ss)
    pair_panel, ss, rest = pair_stage(place_pairs, place_quads, l_pair, inverse, rs, other_rs, rr, other_rr)
    other_ss, rs, rr, other_rs, other_rr = exchange(ss, rest, "gy")
    l_quad, inverse = factor_stage(ss, other_ss)
    quad_panel, quad_update = quad_stage(place_quads, l_quad, inverse, rs, other_rs, rr, other_rr)
    return pair_panel, quad_panel, quad_update


def solution(mesh):
    spec = P("gx", "gy")
    return jax.shard_map(shards, mesh=mesh, in_specs=(spec,) * 3, out_specs=(spec,) * 3, check_vma=False)
```

time: 784 us -> 160 us (0.20); the launches traced: 774 us -> 160 us
  other arithmetic: 366 us -> 0 us
  matrix products: 127 us -> 0 us
  waiting for transfers between devices: 165 us -> 45.9 us
  Pallas kernels: 0 us -> 96.4 us
  local copies, waits for them, and re-layouts: 98.2 us -> 2.46 us
  between operations: 9.6 us -> 0.66 us
    another operation x51 -> x0, other arithmetic: 358 us -> none  [the longest x30 159 us: partial_factor(): corner = jnp.linalg.cholesky(joined[:NS, :NS])]
    ppermute x4 -> x6, waiting for transfers between devices: 165 us -> 45.9 us  [swapped(): lax.ppermute(value, axis, [(i, (i + size // 2) % size) for i in range(siz...]
    pallas_call x0 -> x7, Pallas kernels: none -> 96.4 us  [the longest x2 43.3 us: factor_stage(): pl.pallas_call(factor_kernel, out_shape=(jax.ShapeDtypeStruct((NS, NS), F...]
    dot_general x11 -> x0, matrix products: 93.6 us -> none  [the longest x8 65.4 us: extend_add(): jnp.einsum('ja,aibk,lb->jilk', onehot, blocks, onehot, precision=lax.Prec...]
    unnamed x29 -> x12, local copies, waits for them, and re-layouts: 45.6 us -> 2.46 us
    another operation x39 -> x0, matrix products: 33.5 us -> none  [the longest x14 18.8 us: partial_factor(): jax.scipy.linalg.solve_triangular(corner, joined[:NS, NS:], lower=True)]
    another operation x52 -> x0, local copies, waits for them, and re-layouts: 27.9 us -> none  [the longest x24 19.5 us: partial_factor(): jax.scipy.linalg.solve_triangular(corner, joined[:NS, NS:], lower=True)]
    add x2 -> x0, local copies, waits for them, and re-layouts: 20.7 us -> none  [the longest x1 10.3 us: shards(): extend_add(update_leaf, pair_row)]
  transfers between devices with their start and end apart: 4 -> 6, of which waited for: 2 -> 4; matrix products, arithmetic and copies ran while one was open for 5% -> 0% of each run, Pallas kernels for 0% -> 34%
where the time goes in v1:
time: 160 us
  Pallas kernels  96.4 us (60%)
  waiting for transfers between devices  45.9 us (29%)
  starting transfers between devices  14.1 us (9%)
  local copies, waits for them, and re-layouts  2.46 us (2%)
    ppermute x6, waiting for transfers between devices, swapped(): lax.ppermute(value, axis, [(i, (i + size // 2) % size) for i in range(siz...  45.9 us
    pallas_call x2, Pallas kernels, factor_stage(): pl.pallas_call(factor_kernel, out_shape=(jax.ShapeDtypeStruct((NS, NS), F...  43.3 us
    pallas_call x1, Pallas kernels, leaf_stage(): pl.pallas_call(leaf_solve_kernel, out_shape=(jax.ShapeDtypeStruct((NB, NS...  24.4 us
    ppermute x6, starting transfers between devices, swapped(): lax.ppermute(value, axis, [(i, (i + size // 2) % size) for i in range(siz...  14.1 us
    pallas_call x1, Pallas kernels, quad_stage(): pl.pallas_call(quad_kernel, out_shape=(jax.ShapeDtypeStruct((NJ, NS), F32...  9.9 us
    pallas_call x1, Pallas kernels, pair_stage(): pl.pallas_call(pair_solve_kernel, out_shape=(jax.ShapeDtypeStruct((NJ, NS...  8 us
    pallas_call x1, Pallas kernels, rest(): pl.pallas_call(leaf_rest_kernel, out_shape=(jax.ShapeDtypeStruct((NS, NS)...  6.07 us
    pallas_call x1, Pallas kernels, rest(): pl.pallas_call(pair_rest_kernel, out_shape=(jax.ShapeDtypeStruct((NS, NS)...  4.72 us
  transfers between devices with their start and end apart: 6, of which 4 were waited for; matrix products, arithmetic and copies ran while one was open for 0% of the time, Pallas kernels for 34%

profile of v1, /device:TPU:0, one launch (start us, length us, event | category | flops | bytes accessed | tf_op | source)
XLA Modules:
  0.0 159.6 jit_solution(5927111466042283341)
XLA Ops:
  0.6 24.4 %leaf_solve.1 = (f32[1024,512]{1,0:T(8,128)}, f32[10,128,128]{2,1,0:T(8,128)}) custom-call(s32[1,8]{1,0:T(1,128)} %pair_ref.3, f32[1536,1536]{1,0:T(8,128)} %leaf.3), custom_call_target="tpu_custom_call" | custom-call | flops 10000000000 | bytes 10000000 | tf_op jit(solution)/shard_map/leaf_solve/pallas_call | solution.py:207
  25.1 4.1 %collective-permute-start = (f32[10,128,128]{2,1,0:T(8,128)}, f32[10,128,128]{2,1,0:T(8,128)S(1)}, u32[]{:S(2)}, u32[]{:S(2)}) collective-permute-start(f32[10,128,128]{2,1,0:T(8,128)} %get-tuple-element.24.own), channel_id=1, source_target_pairs={{0,64},{16,80},{32,96},{48,112},{64,0},{80,16},{96,32},{112,48},{1... | collective-permute-start | bytes 1966088 | tf_op jit(solution)/shard_map/ppermute | solution.py:385
  29.1 6.1 %leaf_rest.1 = (f32[512,512]{1,0:T(8,128)}, f32[10,128,128]{2,1,0:T(8,128)}) custom-call(s32[1,8]{1,0:T(1,128)} %pair_ref.3, f32[1536,1536]{1,0:T(8,128)} %leaf.3, f32[1024,512]{1,0:T(8,128)} %get-tuple-element.25.vt), custom_call_target="tpu_custom_call" | custom-call | flops 3000000000 | bytes 10000000 | tf_op jit(solution)/shard_map/leaf_rest/pallas_call | solution.py:225
  35.2 8.9 %collective-permute-done.other = f32[10,128,128]{2,1,0:T(8,128)S(1)} collective-permute-done((f32[10,128,128]{2,1,0:T(8,128)}, f32[10,128,128]{2,1,0:T(8,128)S(1)}, u32[]{:S(2)}, u32[]{:S(2)}) %collective-permute-start) | collective-permute-done | bytes 655392 | tf_op jit(solution)/shard_map/ppermute | solution.py:385
  44.1 3.2 %collective-permute-start.1 = (f32[512,512]{1,0:T(8,128)}, f32[512,512]{1,0:T(8,128)S(1)}, u32[]{:S(2)}, u32[]{:S(2)}) collective-permute-start(f32[512,512]{1,0:T(8,128)} %get-tuple-element.31.rs_own), channel_id=1, source_target_pairs={{0,64},{16,80},{32,96},{48,112},{64,0},{80,16},{96,32},{112,48},{1... | collective-permute-start | bytes 3145736 | tf_op jit(solution)/shard_map/ppermute | solution.py:385
  47.3 0.3 collective-permute-start.2
  47.6 0.0 copy-done.4
  47.6 21.7 %factor.2 = (f32[512,512]{1,0:T(8,128)}, f32[512,512]{1,0:T(8,128)}) custom-call(f32[10,128,128]{2,1,0:T(8,128)} %get-tuple-element.24.own, f32[10,128,128]{2,1,0:T(8,128)} %copy-done.4), custom_call_target="tpu_custom_call" | custom-call | flops 10000000000 | bytes 4000000 | tf_op jit(solution)/shard_map/factor/pallas_call | solution.py:250
  69.3 14.9 %collective-permute-done.2.rr_other = f32[10,128,128]{2,1,0:T(8,128)S(1)} collective-permute-done((f32[10,128,128]{2,1,0:T(8,128)}, f32[10,128,128]{2,1,0:T(8,128)S(1)}, u32[]{:S(2)}, u32[]{:S(2)}) %collective-permute-start.2) | collective-permute-done | bytes 655392 | tf_op jit(solution)/shard_map/ppermute | solution.py:385
  84.2 0.0 collective-permute-done.1.rs_other
  84.2 0.8 copy-done.2
  85.0 0.4 copy-done
  85.4 8.0 %pair_solve.1 = (f32[1536,512]{1,0:T(8,128)}, f32[1024,512]{1,0:T(8,128)}, f32[10,128,128]{2,1,0:T(8,128)}) custom-call(s32[1,8]{1,0:T(1,128)} %pair_ref.3, s32[1,8]{1,0:T(1,128)} %quad_ref.5, f32[512,512]{1,0:T(8,128)} %get-tuple-element.29.l_ref, f32[512,512]{1,0:T(8,128)} %get-tuple-element.30.inverse, f32[512,512]{1,0:T(8,128)} %get-tuple-element.31.rs_own, ...), custom_call_target="tpu_custom_call" | custom-call | flops 3000000000 | bytes 10000000 | tf_op jit(solution)/shard_map/pair_solve/pallas_call | solution.py:319
  93.4 3.0 %collective-permute-start.3 = (f32[10,128,128]{2,1,0:T(8,128)}, f32[10,128,128]{2,1,0:T(8,128)S(1)}, u32[]{:S(2)}, u32[]{:S(2)}) collective-permute-start(f32[10,128,128]{2,1,0:T(8,128)} %get-tuple-element.34.own), channel_id=1, source_target_pairs={{0,8},{1,9},{2,10},{3,11},{4,12},{5,13},{6,14},{7,15},{8,0},{9,1},... | collective-permute-start | bytes 1966088 | tf_op jit(solution)/shard_map/ppermute | solution.py:385
  96.4 4.7 %pair_rest.1 = (f32[512,512]{1,0:T(8,128)}, f32[10,128,128]{2,1,0:T(8,128)}) custom-call(s32[1,8]{1,0:T(1,128)} %pair_ref.3, s32[1,8]{1,0:T(1,128)} %quad_ref.5, f32[1024,512]{1,0:T(8,128)} %get-tuple-element.35.vt, f32[10,128,128]{2,1,0:T(8,128)} %get-tuple-element.32.rr_own, f32[10,128,128]{2,1,0:T(8,128)} %copy-done.2), custom_call_target="tpu_custom_call" | custom-call | flops 3000000000 | bytes 10000000 | tf_op jit(solution)/shard_map/pair_rest/pallas_call | solution.py:334
  101.1 9.0 %collective-permute-done.3.other = f32[10,128,128]{2,1,0:T(8,128)S(1)} collective-permute-done((f32[10,128,128]{2,1,0:T(8,128)}, f32[10,128,128]{2,1,0:T(8,128)S(1)}, u32[]{:S(2)}, u32[]{:S(2)}) %collective-permute-start.3) | collective-permute-done | bytes 655392 | tf_op jit(solution)/shard_map/ppermute | solution.py:385
  110.1 3.0 %collective-permute-start.4 = (f32[512,512]{1,0:T(8,128)}, f32[512,512]{1,0:T(8,128)S(1)}, u32[]{:S(2)}, u32[]{:S(2)}) collective-permute-start(f32[512,512]{1,0:T(8,128)} %get-tuple-element.41.rs_own), channel_id=1, source_target_pairs={{0,8},{1,9},{2,10},{3,11},{4,12},{5,13},{6,14},{7,15},{8,0},{9,1},... | collective-permute-start | bytes 3145736 | tf_op jit(solution)/shard_map/ppermute | solution.py:385
  113.1 0.5 collective-permute-start.5
  113.7 21.6 %factor.3 = (f32[512,512]{1,0:T(8,128)}, f32[512,512]{1,0:T(8,128)}) custom-call(f32[10,128,128]{2,1,0:T(8,128)} %get-tuple-element.34.own, f32[10,128,128]{2,1,0:T(8,128)} %copy-done.3), custom_call_target="tpu_custom_call" | custom-call | flops 10000000000 | bytes 4000000 | tf_op jit(solution)/shard_map/factor/pallas_call | solution.py:250
  135.3 13.2 %collective-permute-done.5.rr_other = f32[10,128,128]{2,1,0:T(8,128)S(1)} collective-permute-done((f32[10,128,128]{2,1,0:T(8,128)}, f32[10,128,128]{2,1,0:T(8,128)S(1)}, u32[]{:S(2)}, u32[]{:S(2)}) %collective-permute-start.5) | collective-permute-done | bytes 655392 | tf_op jit(solution)/shard_map/ppermute | solution.py:385
  148.5 0.0 collective-permute-done.4.rs_other
  148.5 0.8 copy-done.5
  149.3 0.4 copy-done.1
  149.7 9.9 %quad.1 = (f32[1536,512]{1,0:T(8,128)}, f32[1024,1024]{1,0:T(8,128)}) custom-call(s32[1,8]{1,0:T(1,128)} %quad_ref.5, f32[512,512]{1,0:T(8,128)} %get-tuple-element.39.l_ref, f32[512,512]{1,0:T(8,128)} %get-tuple-element.40.inverse, f32[512,512]{1,0:T(8,128)} %get-tuple-element.41.rs_own, f32[512,512]{1,0:T(8,128)} %copy-done.1, ...), custom_call_target="tpu_custom_call" | custom-call | flops 4000000000 | bytes 10000000 | tf_op jit(solution)/shard_map/quad/pallas_call | solution.py:372
  (7 shorter events, 0.0 us)
Async XLA Ops:
  25.1 19.0 %collective-permute-start = (f32[10,128,128]{2,1,0:T(8,128)}, f32[10,128,128]{2,1,0:T(8,128)S(1)}, u32[]{:S(2)}, u32[]{:S(2)}) collective-permute-start(f32[10,128,128]{2,1,0:T(8,128)} %get-tuple-element.24.own), channel_id=1, source_target_pairs={{0,64},{16,80},{32,96},{48,112},{64,0},{80,16},{96,32},{112,48},{1... | collective-permute-start | bytes 1966088 | tf_op jit(solution)/shard_map/ppermute | solution.py:385
  44.1 3.5 %copy-start.4 = (f32[10,128,128]{2,1,0:T(8,128)}, f32[10,128,128]{2,1,0:T(8,128)S(1)}, u32[]{:S(2)}) copy-start(f32[10,128,128]{2,1,0:T(8,128)S(1)} %collective-permute-done.other) | copy-start | bytes 1966084
  44.1 40.1 %collective-permute-start.1 = (f32[512,512]{1,0:T(8,128)}, f32[512,512]{1,0:T(8,128)S(1)}, u32[]{:S(2)}, u32[]{:S(2)}) collective-permute-start(f32[512,512]{1,0:T(8,128)} %get-tuple-element.31.rs_own), channel_id=1, source_target_pairs={{0,64},{16,80},{32,96},{48,112},{64,0},{80,16},{96,32},{112,48},{1... | collective-permute-start | bytes 3145736 | tf_op jit(solution)/shard_map/ppermute | solution.py:385
  47.3 36.8 %collective-permute-start.2 = (f32[10,128,128]{2,1,0:T(8,128)}, f32[10,128,128]{2,1,0:T(8,128)S(1)}, u32[]{:S(2)}, u32[]{:S(2)}) collective-permute-start(f32[10,128,128]{2,1,0:T(8,128)} %get-tuple-element.32.rr_own), channel_id=1, source_target_pairs={{0,64},{16,80},{32,96},{48,112},{64,0},{80,16},{96,32},{112,48},{1... | collective-permute-start | bytes 1966088 | tf_op jit(solution)/shard_map/ppermute | solution.py:385
  84.2 0.8 copy-start.2
  84.2 1.2 copy-start
  93.4 16.8 %collective-permute-start.3 = (f32[10,128,128]{2,1,0:T(8,128)}, f32[10,128,128]{2,1,0:T(8,128)S(1)}, u32[]{:S(2)}, u32[]{:S(2)}) collective-permute-start(f32[10,128,128]{2,1,0:T(8,128)} %get-tuple-element.34.own), channel_id=1, source_target_pairs={{0,8},{1,9},{2,10},{3,11},{4,12},{5,13},{6,14},{7,15},{8,0},{9,1},... | collective-permute-start | bytes 1966088 | tf_op jit(solution)/shard_map/ppermute | solution.py:385
  110.1 3.5 %copy-start.3 = (f32[10,128,128]{2,1,0:T(8,128)}, f32[10,128,128]{2,1,0:T(8,128)S(1)}, u32[]{:S(2)}) copy-start(f32[10,128,128]{2,1,0:T(8,128)S(1)} %collective-permute-done.3.other) | copy-start | bytes 1966084
  110.1 38.4 %collective-permute-start.4 = (f32[512,512]{1,0:T(8,128)}, f32[512,512]{1,0:T(8,128)S(1)}, u32[]{:S(2)}, u32[]{:S(2)}) collective-permute-start(f32[512,512]{1,0:T(8,128)} %get-tuple-element.41.rs_own), channel_id=1, source_target_pairs={{0,8},{1,9},{2,10},{3,11},{4,12},{5,13},{6,14},{7,15},{8,0},{9,1},... | collective-permute-start | bytes 3145736 | tf_op jit(solution)/shard_map/ppermute | solution.py:385
  113.1 35.4 %collective-permute-start.5 = (f32[10,128,128]{2,1,0:T(8,128)}, f32[10,128,128]{2,1,0:T(8,128)S(1)}, u32[]{:S(2)}, u32[]{:S(2)}) collective-permute-start(f32[10,128,128]{2,1,0:T(8,128)} %get-tuple-element.42.rr_own), channel_id=1, source_target_pairs={{0,8},{1,9},{2,10},{3,11},{4,12},{5,13},{6,14},{7,15},{8,0},{9,1},... | collective-permute-start | bytes 1966088 | tf_op jit(solution)/shard_map/ppermute | solution.py:385
  148.5 0.8 copy-start.5
  148.5 1.3 copy-start.1

commit v2 on v1

--- a/solution.py
+++ b/solution.py
@@ -16,7 +16,7 @@
 LOWER = [(a, b) for a in range(4) for b in range(a + 1)]
 VMEM = pl.BlockSpec(memory_space=pltpu.VMEM)
 SMEM = pl.BlockSpec(memory_space=pltpu.SMEM)
-ANY = pl.BlockSpec(memory_space=pl.ANY)
+ANY = pl.BlockSpec(memory_space=pltpu.HBM)
 
 
 def full(x):
@@ -156,21 +156,19 @@
     for copy in copies:
         copy.wait()
     solve_rows(bt, g[:, NS:NB], vt, lambda i, rows: None)
-    sep_update(vt, ss, lambda t: base[t])
-
-
-def sep_update(vt, out, base):
-    v2 = split(vt[0:NS, :])
+    sep_product(split(vt[0:NS, :]), setter(ss, lambda t, block: base[t] - block))
+
+
+def sep_product(v2, put):
     for h in range(2):
         rows = slice(256 * h, 256 * (h + 1))
         prod = dot3((v2[0][rows], v2[1][rows]), (v2[0][0 : 256 * (h + 1)], v2[1][0 : 256 * (h + 1)]), NT)
         for t, (a, b) in enumerate(LOWER):
             if a // 2 == h:
-                out[t] = base(t) - prod[B * (a % 2) : B * (a % 2) + B, B * b : B * b + B]
-
-
-def rest_update(vt, rs, rr, rs_base, rr_base):
-    v2 = split(vt[...])
+                put(t, prod[B * (a % 2) : B * (a % 2) + B, B * b : B * b + B])
+
+
+def rest_product(v2, put_rs, put_rr):
     for h in range(2):
         rows = slice(NS + 256 * h, NS + 256 * (h + 1))
         last = NS + 256 * (h + 1)
@@ -178,10 +176,24 @@
         for a in (2 * h, 2 * h + 1):
             r = B * (a % 2)
             for b in range(4):
-                rs[B * a : B * a + B, B * b : B * b + B] = rs_base(a, b) - prod[r : r + B, B * b : B * b + B]
+                put_rs(a, b, prod[r : r + B, B * b : B * b + B])
         for t, (a, b) in enumerate(LOWER):
             if a // 2 == h:
-                rr[t] = rr_base(t) - prod[B * (a % 2) : B * (a % 2) + B, NS + B * b : NS + B * b + B]
+                put_rr(t, prod[B * (a % 2) : B * (a % 2) + B, NS + B * b : NS + B * b + B])
+
+
+def setter(ref, value):
+    def put(t, block):
+        ref[t] = value(t, block)
+
+    return put
+
+
+def rs_setter(ref, value):
+    def put(a, b, block):
+        ref[B * a : B * a + B, B * b : B * b + B] = value(a, b, block)
+
+    return put
 
 
 def leaf_rest_kernel(place_ref, leaf, vt, rs, rr, rs_buf, rr_buf, sems):
@@ -200,7 +212,11 @@
         copy.start()
     for copy in copies:
         copy.wait()
-    rest_update(vt, rs, rr, lambda a, b: rs_buf[4 * a + b], lambda t: rr_buf[t])
+    rest_product(
+        split(vt[...]),
+        rs_setter(rs, lambda a, b, block: rs_buf[4 * a + b] - block),
+        setter(rr, lambda t, block: rr_buf[t] - block),
+    )
 
 
 def leaf_stage(leaf, place):
@@ -218,6 +234,7 @@
             pltpu.SemaphoreType.DMA((19,)),
         ],
         cost_estimate=pl.CostEstimate(flops=10**10, bytes_accessed=10**7, transcendentals=0),
+        compiler_params=pltpu.CompilerParams(vmem_limit_bytes=54 * 2**20),
         name="leaf_solve",
     )(place, leaf)
 
@@ -229,6 +246,7 @@
             out_specs=(VMEM, VMEM),
             scratch_shapes=[pltpu.VMEM((16, B, B), F32), pltpu.VMEM((10, B, B), F32), pltpu.SemaphoreType.DMA((26,))],
             cost_estimate=pl.CostEstimate(flops=3 * 10**9, bytes_accessed=10**7, transcendentals=0),
+            compiler_params=pltpu.CompilerParams(vmem_limit_bytes=54 * 2**20),
             name="leaf_rest",
         )(place, leaf, vt)
 
@@ -254,6 +272,7 @@
         out_specs=(VMEM, VMEM),
         scratch_shapes=[pltpu.VMEM((NS, NB), F32), pltpu.VMEM((B, 2 * B), F32)],
         cost_estimate=pl.CostEstimate(flops=10**10, bytes_accessed=4 * 10**6, transcendentals=0),
+        compiler_params=pltpu.CompilerParams(vmem_limit_bytes=16 * 2**20),
         name="factor",
     )(own, other)
 
@@ -286,10 +305,14 @@
     return jnp.where(same, jnp.where(sa < 4, 0, 16) + 4 * (sa % 4) + sb % 4, 32)
 
 
-def pair_solve_kernel(pair_ref, quad_ref, l_ref, inverse, rs_own, rs_other, rr_own, rr_other, panel, vt, ss, blocks, bt):
+def pair_order(pair_ref, quad_ref):
     order = order_of([quad_ref[0, i] for i in range(8)])
     where = source_of([pair_ref[0, i] for i in range(8)])
-    source = [sum(jnp.where(order[a] == u, where[u], 0) for u in range(8)) for a in range(8)]
+    return order, [sum(jnp.where(order[a] == u, where[u], 0) for u in range(8)) for a in range(8)]
+
+
+def pair_solve_kernel(pair_ref, quad_ref, l_ref, inverse, rs_own, rs_other, panel, ss, rs, rr, bt, vt):
+    order, source = pair_order(pair_ref, quad_ref)
     gather_rows(rs_own, rs_other, source, bt)
     panel[0:NS, :] = l_ref[...]
 
@@ -297,54 +320,57 @@
         panel[pl.ds(pl.multiple_of(NS + B * order[i], B), B), :] = rows
 
     solve_rows(bt, inverse[...], vt, store)
+    v2 = split(vt[...])
+    sep_product(v2, setter(ss, lambda t, block: block))
+    rest_product(v2, rs_setter(rs, lambda a, b, block: block), setter(rr, lambda t, block: block))
+
+
+def pair_update_kernel(pair_ref, quad_ref, ss_in, rs_in, rr_in, rr_own, rr_other, ss, rs, rr, blocks):
+    _, source = pair_order(pair_ref, quad_ref)
     spread_rest(rr_own, rr_other, blocks)
-    sep_update(vt, ss, lambda t: blocks[block_at(source, *LOWER[t])])
-
-
-def pair_rest_kernel(pair_ref, quad_ref, vt, rr_own, rr_other, rs, rr, blocks):
-    order = order_of([quad_ref[0, i] for i in range(8)])
-    where = source_of([pair_ref[0, i] for i in range(8)])
-    source = [sum(jnp.where(order[a] == u, where[u], 0) for u in range(8)) for a in range(8)]
-    spread_rest(rr_own, rr_other, blocks)
-    rest_update(
-        vt,
-        rs,
-        rr,
-        lambda a, b: blocks[block_at(source, 4 + a, b)],
-        lambda t: blocks[block_at(source, 4 + LOWER[t][0], 4 + LOWER[t][1])],
-    )
+    for t, (a, b) in enumerate(LOWER):
+        ss[t] = blocks[block_at(source, a, b)] - ss_in[t]
+        rr[t] = blocks[block_at(source, 4 + a, 4 + b)] - rr_in[t]
+    for a in range(4):
+        for b in range(4):
+            at = (slice(B * a, B * a + B), slice(B * b, B * b + B))
+            rs[at] = blocks[block_at(source, 4 + a, b)] - rs_in[at]
+
+
+LOWER10 = jax.ShapeDtypeStruct((10, B, B), F32)
+SQUARE = jax.ShapeDtypeStruct((NS, NS), F32)
+PANEL = jax.ShapeDtypeStruct((NJ, NS), F32)
+
+
+def params(mib):
+    return pltpu.CompilerParams(vmem_limit_bytes=mib * 2**20)
 
 
 def pair_stage(pair, quad, l_full, inverse, rs_own, rs_other, rr_own, rr_other):
-    panel, vt, ss = pl.pallas_call(
+    panel, ss, rs, rr = pl.pallas_call(
         pair_solve_kernel,
-        out_shape=(
-            jax.ShapeDtypeStruct((NJ, NS), F32),
-            jax.ShapeDtypeStruct((NB, NS), F32),
-            jax.ShapeDtypeStruct((10, B, B), F32),
-        ),
-        in_specs=[SMEM, SMEM] + [VMEM] * 6,
-        out_specs=(VMEM,) * 3,
-        scratch_shapes=[pltpu.VMEM((33, B, B), F32), pltpu.VMEM((NB, NS), F32)],
+        out_shape=(PANEL, LOWER10, SQUARE, LOWER10),
+        in_specs=[SMEM, SMEM] + [VMEM] * 4,
+        out_specs=(VMEM,) * 4,
+        scratch_shapes=[pltpu.VMEM((NB, NS), F32), pltpu.VMEM((NB, NS), F32)],
+        compiler_params=params(32),
         cost_estimate=pl.CostEstimate(flops=3 * 10**9, bytes_accessed=10**7, transcendentals=0),
         name="pair_solve",
-    )(pair, quad, l_full, inverse, rs_own, rs_other, rr_own, rr_other)
-
-    def rest():
-        return pl.pallas_call(
-            pair_rest_kernel,
-            out_shape=(jax.ShapeDtypeStruct((NS, NS), F32), jax.ShapeDtypeStruct((10, B, B), F32)),
-            in_specs=[SMEM, SMEM] + [VMEM] * 3,
-            out_specs=(VMEM, VMEM),
-            scratch_shapes=[pltpu.VMEM((33, B, B), F32)],
-            cost_estimate=pl.CostEstimate(flops=3 * 10**9, bytes_accessed=10**7, transcendentals=0),
-            name="pair_rest",
-        )(pair, quad, vt, rr_own, rr_other)
-
-    return panel, ss, rest
-
-
-def quad_kernel(quad_ref, l_ref, inverse, rs_own, rs_other, rr_own, rr_other, panel, update, blocks, bt, vt):
+    )(pair, quad, l_full, inverse, rs_own, rs_other)
+    ss, rs, rr = pl.pallas_call(
+        pair_update_kernel,
+        out_shape=(LOWER10, SQUARE, LOWER10),
+        in_specs=[SMEM, SMEM] + [VMEM] * 5,
+        out_specs=(VMEM,) * 3,
+        scratch_shapes=[pltpu.VMEM((33, B, B), F32)],
+        compiler_params=params(24),
+        cost_estimate=pl.CostEstimate(flops=10**6, bytes_accessed=10**7, transcendentals=0),
+        name="pair_update",
+    )(pair, quad, ss, rs, rr, rr_own, rr_other)
+    return panel, ss, rs, rr
+
+
+def quad_solve_kernel(quad_ref, l_ref, inverse, rs_own, rs_other, panel, lower, bt, vt):
     source = source_of([quad_ref[0, i] for i in range(8)])
     gather_rows(rs_own, rs_other, source, bt)
     panel[0:NS, :] = l_ref[...]
@@ -353,31 +379,46 @@
         panel[NS + B * i : NS + B * i + B, :] = rows
 
     solve_rows(bt, inverse[...], vt, store)
-    spread_rest(rr_own, rr_other, blocks)
     v2 = split(vt[...])
     for h in range(4):
         rows = slice(256 * h, 256 * (h + 1))
         last = 256 * (h + 1)
-        prod = dot3((v2[0][rows], v2[1][rows]), (v2[0][0:last], v2[1][0:last]), NT)
-        for a in (2 * h, 2 * h + 1):
-            r = B * (a % 2)
-            for b in range(a + 1):
-                block = blocks[block_at(source, a, b)] - prod[r : r + B, B * b : B * b + B]
-                update[B * a : B * a + B, B * b : B * b + B] = block
-                if a != b:
-                    update[B * b : B * b + B, B * a : B * a + B] = block.T
+        lower[rows, 0:last] = dot3((v2[0][rows], v2[1][rows]), (v2[0][0:last], v2[1][0:last]), NT)
+
+
+def quad_update_kernel(quad_ref, lower, rr_own, rr_other, update, blocks):
+    source = source_of([quad_ref[0, i] for i in range(8)])
+    spread_rest(rr_own, rr_other, blocks)
+    for a in range(8):
+        for b in range(a + 1):
+            block = blocks[block_at(source, a, b)] - lower[B * a : B * a + B, B * b : B * b + B]
+            update[B * a : B * a + B, B * b : B * b + B] = block
+            if a != b:
+                update[B * b : B * b + B, B * a : B * a + B] = block.T
 
 
 def quad_stage(quad, l_full, inverse, rs_own, rs_other, rr_own, rr_other):
-    return pl.pallas_call(
-        quad_kernel,
-        out_shape=(jax.ShapeDtypeStruct((NJ, NS), F32), jax.ShapeDtypeStruct((NB, NB), F32)),
-        in_specs=[SMEM] + [VMEM] * 6,
+    panel, lower = pl.pallas_call(
+        quad_solve_kernel,
+        out_shape=(PANEL, jax.ShapeDtypeStruct((NB, NB), F32)),
+        in_specs=[SMEM] + [VMEM] * 4,
         out_specs=(VMEM, VMEM),
-        scratch_shapes=[pltpu.VMEM((33, B, B), F32), pltpu.VMEM((NB, NS), F32), pltpu.VMEM((NB, NS), F32)],
+        scratch_shapes=[pltpu.VMEM((NB, NS), F32), pltpu.VMEM((NB, NS), F32)],
+        compiler_params=params(32),
         cost_estimate=pl.CostEstimate(flops=4 * 10**9, bytes_accessed=10**7, transcendentals=0),
-        name="quad",
-    )(quad, l_full, inverse, rs_own, rs_other, rr_own, rr_other)
+        name="quad_solve",
+    )(quad, l_full, inverse, rs_own, rs_other)
+    update = pl.pallas_call(
+        quad_update_kernel,
+        out_shape=jax.ShapeDtypeStruct((NB, NB), F32),
+        in_specs=[SMEM] + [VMEM] * 3,
+        out_specs=VMEM,
+        scratch_shapes=[pltpu.VMEM((33, B, B), F32)],
+        compiler_params=params(24),
+        cost_estimate=pl.CostEstimate(flops=10**6, bytes_accessed=10**7, transcendentals=0),
+        name="quad_update",
+    )(quad, lower, rr_own, rr_other)
+    return panel, update
 
 
 def swapped(value, axis):
@@ -385,19 +426,14 @@
     return lax.ppermute(value, axis, [(i, (i + size // 2) % size) for i in range(size)])
 
 
-def exchange(ss, rest, axis):
-    other_ss = swapped(ss, axis)
-    rs, rr = rest()
-    other_ss, rs_late, rr_late = lax.optimization_barrier((other_ss, rs, rr))
-    return other_ss, rs, rr, swapped(rs_late, axis), swapped(rr_late, axis)
-
-
 def shards(leaf_front, place_pairs, place_quads):
     ss, rest = leaf_stage(leaf_front, place_pairs)
-    other_ss, rs, rr, other_rs, other_rr = exchange(ss, rest, "gx")
+    other_ss = swapped(ss, "gx")
+    rs, rr = rest()
+    other_rs, other_rr = swapped(rs, "gx"), swapped(rr, "gx")
     l_pair, inverse = factor_stage(ss, other_ss)
-    pair_panel, ss, rest = pair_stage(place_pairs, place_quads, l_pair, inverse, rs, other_rs, rr, other_rr)
-    other_ss, rs, rr, other_rs, other_rr = exchange(ss, rest, "gy")
+    pair_panel, ss, rs, rr = pair_stage(place_pairs, place_quads, l_pair, inverse, rs, other_rs, rr, other_rr)
+    other_ss, other_rs, other_rr = swapped(ss, "gy"), swapped(rs, "gy"), swapped(rr, "gy")
     l_quad, inverse = factor_stage(ss, other_ss)
     quad_panel, quad_update = quad_stage(place_quads, l_quad, inverse, rs, other_rs, rr, other_rr)
     return pair_panel, quad_panel, quad_update

time: 160 us -> 140 us (0.88)
  Pallas kernels: 96.4 us -> 86.7 us
  waiting for transfers between devices: 45.9 us -> 37.8 us
  local copies, waits for them, and re-layouts: 2.46 us -> 0.02 us
    ppermute x6, waiting for transfers between devices: 45.9 us -> 37.8 us  [swapped(): lax.ppermute(value, axis, [(i, (i + size // 2) % size) for i in range(siz...]
    pallas_call x2, Pallas kernels: 43.3 us -> 38.2 us  [factor_stage(): pl.pallas_call(factor_kernel, out_shape=(jax.ShapeDtypeStruct((NS, NS), F...]
    pallas_call x3 -> x4, Pallas kernels: 22.6 us -> 17.9 us  [the longest x1 6.57 us: pair_stage(): pl.pallas_call(pair_solve_kernel, out_shape=(PANEL, LOWER10, SQUARE, LOWE...]
    unnamed x12 -> x10, local copies, waits for them, and re-layouts: 2.46 us -> 0.02 us
  transfers between devices with their start and end apart: 6 -> 6, of which waited for: 4 -> 6; matrix products, arithmetic and copies ran while one was open for 0% -> 0% of each run, Pallas kernels for 34% -> 41%
where the time goes in v2:
time: 140 us
  Pallas kernels  86.7 us (62%)
  waiting for transfers between devices  37.8 us (27%)
  starting transfers between devices  14.3 us (10%)
    pallas_call x2, Pallas kernels, factor_stage(): pl.pallas_call(factor_kernel, out_shape=(jax.ShapeDtypeStruct((NS, NS), F...  38.2 us
    ppermute x6, waiting for transfers between devices, swapped(): lax.ppermute(value, axis, [(i, (i + size // 2) % size) for i in range(siz...  37.8 us
    pallas_call x1, Pallas kernels, leaf_stage(): pl.pallas_call(leaf_solve_kernel, out_shape=(jax.ShapeDtypeStruct((NB, NS...  24.4 us
    ppermute x6, starting transfers between devices, swapped(): lax.ppermute(value, axis, [(i, (i + size // 2) % size) for i in range(siz...  14.3 us
    pallas_call x1, Pallas kernels, pair_stage(): pl.pallas_call(pair_solve_kernel, out_shape=(PANEL, LOWER10, SQUARE, LOWE...  6.57 us
    pallas_call x1, Pallas kernels, quad_stage(): pl.pallas_call(quad_solve_kernel, out_shape=(PANEL, jax.ShapeDtypeStruct(...  6.41 us
    pallas_call x1, Pallas kernels, rest(): pl.pallas_call(leaf_rest_kernel, out_shape=(jax.ShapeDtypeStruct((NS, NS)...  6.12 us
    pallas_call x1, Pallas kernels, quad_stage(): pl.pallas_call(quad_update_kernel, out_shape=jax.ShapeDtypeStruct((NB, NB...  3.58 us
  transfers between devices with their start and end apart: 6, of which 6 were waited for; matrix products, arithmetic and copies ran while one was open for 0% of the time, Pallas kernels for 41%

profile of v2, /device:TPU:0, one launch (start us, length us, event | category | flops | bytes accessed | tf_op | source)
XLA Modules:
  0.0 139.5 jit_solution(639603477835790274)
XLA Ops:
  0.6 24.4 %leaf_solve.1 = (f32[1024,512]{1,0:T(8,128)}, f32[10,128,128]{2,1,0:T(8,128)}) custom-call(s32[1,8]{1,0:T(1,128)} %pair_ref.3, f32[1536,1536]{1,0:T(8,128)} %leaf.3), custom_call_target="tpu_custom_call" | custom-call | flops 10000000000 | bytes 10000000 | tf_op jit(solution)/shard_map/leaf_solve/pallas_call | solution.py:223
  25.1 4.1 %collective-permute-start = (f32[10,128,128]{2,1,0:T(8,128)}, f32[10,128,128]{2,1,0:T(8,128)S(1)}, u32[]{:S(2)}, u32[]{:S(2)}) collective-permute-start(f32[10,128,128]{2,1,0:T(8,128)} %get-tuple-element.20.own), channel_id=1, source_target_pairs={{0,64},{16,80},{32,96},{48,112},{64,0},{80,16},{96,32},{112,48},{1... | collective-permute-start | bytes 1966088 | tf_op jit(solution)/shard_map/ppermute | solution.py:426
  29.1 6.1 %leaf_rest.1 = (f32[512,512]{1,0:T(8,128)}, f32[10,128,128]{2,1,0:T(8,128)}) custom-call(s32[1,8]{1,0:T(1,128)} %pair_ref.3, f32[1536,1536]{1,0:T(8,128)} %leaf.3, f32[1024,512]{1,0:T(8,128)} %get-tuple-element.23.vt), custom_call_target="tpu_custom_call" | custom-call | flops 3000000000 | bytes 10000000 | tf_op jit(solution)/shard_map/leaf_rest/pallas_call | solution.py:242
  35.3 0.1 collective-permute-start.1
  35.4 0.0 copy-start.2
  35.4 0.0 copy-start.3
  35.4 3.5 %collective-permute-start.2 = (f32[10,128,128]{2,1,0:T(8,128)}, f32[10,128,128]{2,1,0:T(8,128)S(1)}, u32[]{:S(2)}, u32[]{:S(2)}) collective-permute-start(f32[10,128,128]{2,1,0:T(8,128)} %get-tuple-element.29.rr_own), channel_id=1, source_target_pairs={{0,64},{16,80},{32,96},{48,112},{64,0},{80,16},{96,32},{112,48},{1... | collective-permute-start | bytes 1966088 | tf_op jit(solution)/shard_map/ppermute | solution.py:426
  38.9 6.0 %collective-permute-done.other = f32[10,128,128]{2,1,0:T(8,128)S(1)} collective-permute-done((f32[10,128,128]{2,1,0:T(8,128)}, f32[10,128,128]{2,1,0:T(8,128)S(1)}, u32[]{:S(2)}, u32[]{:S(2)}) %collective-permute-start) | collective-permute-done | bytes 655392 | tf_op jit(solution)/shard_map/ppermute | solution.py:426
  44.9 0.0 copy-done.4
  44.9 19.1 %factor.2 = (f32[512,512]{1,0:T(8,128)S(1)}, f32[512,512]{1,0:T(8,128)S(1)}) custom-call(f32[10,128,128]{2,1,0:T(8,128)S(1)} %copy-done.4, f32[10,128,128]{2,1,0:T(8,128)S(1)} %collective-permute-done.other), custom_call_target="tpu_custom_call" | custom-call | flops 10000000000 | bytes 4000000 | tf_op jit(solution)/shard_map/factor/pallas_call | solution.py:268
  64.0 3.3 %collective-permute-done.1.rs_other = f32[512,512]{1,0:T(8,128)S(1)} collective-permute-done((f32[512,512]{1,0:T(8,128)}, f32[512,512]{1,0:T(8,128)S(1)}, u32[]{:S(2)}, u32[]{:S(2)}) %collective-permute-start.1) | collective-permute-done | bytes 1048608 | tf_op jit(solution)/shard_map/ppermute | solution.py:426
  67.4 0.0 copy-done.3
  67.4 6.6 %pair_solve.1 = (f32[1536,512]{1,0:T(8,128)}, f32[10,128,128]{2,1,0:T(8,128)S(1)}, f32[512,512]{1,0:T(8,128)S(1)}, f32[10,128,128]{2,1,0:T(8,128)S(1)}) custom-call(s32[1,8]{1,0:T(1,128)S(1)} %copy-done.1, s32[1,8]{1,0:T(1,128)S(1)} %copy-done.2, f32[512,512]{1,0:T(8,128)S(1)} %get-tuple-element.21.l_ref, f32[512,512]{1,0:T(8,128)S(1)} %get-tuple-element.22.inverse, ...), custom_call_target="tpu_custom_call" | custom-call | flops 3000000000 | bytes 10000000 | tf_op jit(solution)/shard_map/pair_solve/pallas_call | solution.py:350
  74.0 6.6 %collective-permute-done.2.rr_other = f32[10,128,128]{2,1,0:T(8,128)S(1)} collective-permute-done((f32[10,128,128]{2,1,0:T(8,128)}, f32[10,128,128]{2,1,0:T(8,128)S(1)}, u32[]{:S(2)}, u32[]{:S(2)}) %collective-permute-start.2) | collective-permute-done | bytes 655392 | tf_op jit(solution)/shard_map/ppermute | solution.py:426
  80.6 1.3 pair_update.1
  81.9 3.1 %collective-permute-start.3 = (f32[10,128,128]{2,1,0:T(8,128)S(1)}, f32[10,128,128]{2,1,0:T(8,128)S(1)}, u32[]{:S(2)}, u32[]{:S(2)}) collective-permute-start(f32[10,128,128]{2,1,0:T(8,128)S(1)} %get-tuple-element.30.own), channel_id=1, source_target_pairs={{0,8},{1,9},{2,10},{3,11},{4,12},{5,13},{6,14},{7,15},{8,0},{9,1},... | collective-permute-start | bytes 1966088 | tf_op jit(solution)/shard_map/ppermute | solution.py:426
  85.0 0.5 collective-permute-start.4
  85.5 3.0 %collective-permute-start.5 = (f32[10,128,128]{2,1,0:T(8,128)S(1)}, f32[10,128,128]{2,1,0:T(8,128)S(1)}, u32[]{:S(2)}, u32[]{:S(2)}) collective-permute-start(f32[10,128,128]{2,1,0:T(8,128)S(1)} %get-tuple-element.36.rr_own), channel_id=1, source_target_pairs={{0,8},{1,9},{2,10},{3,11},{4,12},{5,13},{6,14},{7,15},{8,0},{9,1},... | collective-permute-start | bytes 1966088 | tf_op jit(solution)/shard_map/ppermute | solution.py:426
  88.6 12.6 %collective-permute-done.3.other = f32[10,128,128]{2,1,0:T(8,128)S(1)} collective-permute-done((f32[10,128,128]{2,1,0:T(8,128)S(1)}, f32[10,128,128]{2,1,0:T(8,128)S(1)}, u32[]{:S(2)}, u32[]{:S(2)}) %collective-permute-start.3) | collective-permute-done | bytes 655392 | tf_op jit(solution)/shard_map/ppermute | solution.py:426
  101.1 19.1 %factor.3 = (f32[512,512]{1,0:T(8,128)S(1)}, f32[512,512]{1,0:T(8,128)S(1)}) custom-call(f32[10,128,128]{2,1,0:T(8,128)S(1)} %get-tuple-element.30.own, f32[10,128,128]{2,1,0:T(8,128)S(1)} %collective-permute-done.3.other), custom_call_target="tpu_custom_call" | custom-call | flops 10000000000 | bytes 4000000 | tf_op jit(solution)/shard_map/factor/pallas_call | solution.py:268
  120.2 3.3 %collective-permute-done.4.rs_other = f32[512,512]{1,0:T(8,128)S(1)} collective-permute-done((f32[512,512]{1,0:T(8,128)S(1)}, f32[512,512]{1,0:T(8,128)S(1)}, u32[]{:S(2)}, u32[]{:S(2)}) %collective-permute-start.4) | collective-permute-done | bytes 1048608 | tf_op jit(solution)/shard_map/ppermute | solution.py:426
  123.6 6.4 %quad_solve.1 = (f32[1536,512]{1,0:T(8,128)}, f32[1024,1024]{1,0:T(8,128)S(1)}) custom-call(s32[1,8]{1,0:T(1,128)S(1)} %copy-done.2, f32[512,512]{1,0:T(8,128)S(1)} %get-tuple-element.31.l_ref, f32[512,512]{1,0:T(8,128)S(1)} %get-tuple-element.32.inverse, f32[512,512]{1,0:T(8,128)S(1)} %get-tuple-element.33.rs_own, ...), custom_call_target="tpu_custom_call" | custom-call | flops 4000000000 | bytes 10000000 | tf_op jit(solution)/shard_map/quad_solve/pallas_call | solution.py:401
  130.0 5.9 %collective-permute-done.5.rr_other = f32[10,128,128]{2,1,0:T(8,128)S(1)} collective-permute-done((f32[10,128,128]{2,1,0:T(8,128)S(1)}, f32[10,128,128]{2,1,0:T(8,128)S(1)}, u32[]{:S(2)}, u32[]{:S(2)}) %collective-permute-start.5) | collective-permute-done | bytes 655392 | tf_op jit(solution)/shard_map/ppermute | solution.py:426
  135.9 3.6 %quad_update.1 = f32[1024,1024]{1,0:T(8,128)} custom-call(s32[1,8]{1,0:T(1,128)S(1)} %copy-done.2, f32[1024,1024]{1,0:T(8,128)S(1)} %get-tuple-element.35.lower, f32[10,128,128]{2,1,0:T(8,128)S(1)} %get-tuple-element.36.rr_own, f32[10,128,128]{2,1,0:T(8,128)S(1)} %collective-permute-done.5.rr_other), custom_call_target="tpu_custom_call" | custom-call | flops 1000000 | bytes 10000000 | tf_op jit(solution)/shard_map/quad_update/pallas_call | solution.py:411
  (6 shorter events, 0.0 us)
Async XLA Ops:
  25.1 19.9 %collective-permute-start = (f32[10,128,128]{2,1,0:T(8,128)}, f32[10,128,128]{2,1,0:T(8,128)S(1)}, u32[]{:S(2)}, u32[]{:S(2)}) collective-permute-start(f32[10,128,128]{2,1,0:T(8,128)} %get-tuple-element.20.own), channel_id=1, source_target_pairs={{0,64},{16,80},{32,96},{48,112},{64,0},{80,16},{96,32},{112,48},{1... | collective-permute-start | bytes 1966088 | tf_op jit(solution)/shard_map/ppermute | solution.py:426
  29.1 15.8 %copy-start.4 = (f32[10,128,128]{2,1,0:T(8,128)S(1)}, f32[10,128,128]{2,1,0:T(8,128)}, u32[]{:S(2)}) copy-start(f32[10,128,128]{2,1,0:T(8,128)} %get-tuple-element.20.own) | copy-start | bytes 1966084
  35.3 32.1 %collective-permute-start.1 = (f32[512,512]{1,0:T(8,128)}, f32[512,512]{1,0:T(8,128)S(1)}, u32[]{:S(2)}, u32[]{:S(2)}) collective-permute-start(f32[512,512]{1,0:T(8,128)} %get-tuple-element.24.rs_own), channel_id=1, source_target_pairs={{0,64},{16,80},{32,96},{48,112},{64,0},{80,16},{96,32},{112,48},{1... | collective-permute-start | bytes 3145736 | tf_op jit(solution)/shard_map/ppermute | solution.py:426
  35.4 32.0 %copy-start.1 = (s32[1,8]{1,0:T(1,128)S(1)}, s32[1,8]{1,0:T(1,128)}, u32[]{:S(2)}) copy-start(s32[1,8]{1,0:T(1,128)} %pair_ref.3) | copy-start | bytes 100
  35.4 32.0 %copy-start.2 = (s32[1,8]{1,0:T(1,128)S(1)}, s32[1,8]{1,0:T(1,128)}, u32[]{:S(2)}) copy-start(s32[1,8]{1,0:T(1,128)} %quad_ref.7) | copy-start | bytes 100
  35.4 32.0 %copy-start.3 = (f32[512,512]{1,0:T(8,128)S(1)}, f32[512,512]{1,0:T(8,128)}, u32[]{:S(2)}) copy-start(f32[512,512]{1,0:T(8,128)} %get-tuple-element.24.rs_own) | copy-start | bytes 3145732
  35.4 45.2 %collective-permute-start.2 = (f32[10,128,128]{2,1,0:T(8,128)}, f32[10,128,128]{2,1,0:T(8,128)S(1)}, u32[]{:S(2)}, u32[]{:S(2)}) collective-permute-start(f32[10,128,128]{2,1,0:T(8,128)} %get-tuple-element.29.rr_own), channel_id=1, source_target_pairs={{0,64},{16,80},{32,96},{48,112},{64,0},{80,16},{96,32},{112,48},{1... | collective-permute-start | bytes 1966088 | tf_op jit(solution)/shard_map/ppermute | solution.py:426
  67.4 13.2 %copy-start = (f32[10,128,128]{2,1,0:T(8,128)S(1)}, f32[10,128,128]{2,1,0:T(8,128)}, u32[]{:S(2)}) copy-start(f32[10,128,128]{2,1,0:T(8,128)} %get-tuple-element.29.rr_own) | copy-start | bytes 1966084
  81.9 19.2 %collective-permute-start.3 = (f32[10,128,128]{2,1,0:T(8,128)S(1)}, f32[10,128,128]{2,1,0:T(8,128)S(1)}, u32[]{:S(2)}, u32[]{:S(2)}) collective-permute-start(f32[10,128,128]{2,1,0:T(8,128)S(1)} %get-tuple-element.30.own), channel_id=1, source_target_pairs={{0,8},{1,9},{2,10},{3,11},{4,12},{5,13},{6,14},{7,15},{8,0},{9,1},... | collective-permute-start | bytes 1966088 | tf_op jit(solution)/shard_map/ppermute | solution.py:426
  85.0 38.6 %collective-permute-start.4 = (f32[512,512]{1,0:T(8,128)S(1)}, f32[512,512]{1,0:T(8,128)S(1)}, u32[]{:S(2)}, u32[]{:S(2)}) collective-permute-start(f32[512,512]{1,0:T(8,128)S(1)} %get-tuple-element.33.rs_own), channel_id=1, source_target_pairs={{0,8},{1,9},{2,10},{3,11},{4,12},{5,13},{6,14},{7,15},{8,0},{9,1},... | collective-permute-start | bytes 3145736 | tf_op jit(solution)/shard_map/ppermute | solution.py:426
  85.5 50.4 %collective-permute-start.5 = (f32[10,128,128]{2,1,0:T(8,128)S(1)}, f32[10,128,128]{2,1,0:T(8,128)S(1)}, u32[]{:S(2)}, u32[]{:S(2)}) collective-permute-start(f32[10,128,128]{2,1,0:T(8,128)S(1)} %get-tuple-element.36.rr_own), channel_id=1, source_target_pairs={{0,8},{1,9},{2,10},{3,11},{4,12},{5,13},{6,14},{7,15},{8,0},{9,1},... | collective-permute-start | bytes 1966088 | tf_op jit(solution)/shard_map/ppermute | solution.py:426

commit v3 on v2

--- a/solution.py
+++ b/solution.py
@@ -15,6 +15,11 @@
 NJ = 1536
 LOWER = [(a, b) for a in range(4) for b in range(a + 1)]
 VMEM = pl.BlockSpec(memory_space=pltpu.VMEM)
+MESH = pl.DeviceIdType.MESH
+RS0, RR0, BLOCKS = 10, 26, 36
+CHUNKS = [(2 * i, 2) for i in range(5)] + [(RS0 + 4 * i, 4) for i in range(4)] + [(RR0, 4), (RR0 + 4, 6)]
+SEP_CHUNKS = 5
+FORWARD = [(5, 6, 7), (8, 9), (10,), ()]
 SMEM = pl.BlockSpec(memory_space=pltpu.SMEM)
 ANY = pl.BlockSpec(memory_space=pltpu.HBM)
 
@@ -81,7 +86,7 @@
     return i0, i1, jnp.where(i0 == i1, 1.0, 0.0).astype(F32)
 
 
-def factor_front(g, m, l_ref):
+def factor_front(g, m, l_ref, after=lambda step: None):
     i0, i1, eye = eye_block()
     m[:, 0:B] = g[0:B, 0:B]
     m[:, B : 2 * B] = eye
@@ -93,6 +98,7 @@
 
             @pl.when(k == kk)
             def _(kk=kk):
+                after(kk)
                 c, n = B * kk, B * (kk + 1)
                 inverse = m[:, B : 2 * B]
                 l_ref[c:n, c:n] = jnp.where(i0 <= i1, m[:, 0:B], 0.0).T
@@ -254,14 +260,91 @@
 
 
 def factor_kernel(own, other, l_ref, inverse, g, m):
+    joined_separator(own, other, g)
+    factor_front(g, m, l_ref)
+    inverse[...] = g[:, NS:NB]
+
+
+def joined_separator(own, other, g):
     for t, (a, b) in enumerate(LOWER):
         block = own[t] + other[t]
         g[B * a : B * a + B, B * b : B * b + B] = block
         if a != b:
             g[B * b : B * b + B, B * a : B * a + B] = block.T
     g[:, NS:NB] = jnp.zeros((NS, NS), F32)
-    factor_front(g, m, l_ref)
+
+
+def quad_factor_kernel(half_gx, half_gy, own, l_ref, inverse, received, other, g, m, far_send, far_recv, near_send, near_recv):
+    gx, gy = lax.axis_index("gx"), lax.axis_index("gy")
+    side = gx // half_gx
+    far = (gx, lax.rem(gy + half_gy, 2 * half_gy))
+    near = (lax.rem(gx + half_gx, 2 * half_gx), gy)
+    barrier = pltpu.get_barrier_semaphore()
+    for device in (far, near):
+        pl.semaphore_signal(barrier, inc=1, device_id=device, device_id_type=MESH)
+    pl.semaphore_wait(barrier, 2)
+
+    def far_copy(c):
+        start, count = CHUNKS[c]
+        part = pl.ds(start + side * (count // 2), count // 2)
+        return pltpu.make_async_remote_copy(
+            own.at[part], other.at[part], far_send.at[c], far_recv.at[c], device_id=far, device_id_type=MESH
+        )
+
+    def near_copy(c):
+        start, count = CHUNKS[c]
+        part = pl.ds(start + side * (count // 2), count // 2)
+        return pltpu.make_async_remote_copy(
+            other.at[part], other.at[part], near_send.at[c], near_recv.at[c], device_id=near, device_id_type=MESH
+        )
+
+    def forward(c):
+        far_copy(c).wait_recv()
+        near_copy(c).start()
+
+    for c in range(len(CHUNKS)):
+        far_copy(c).start()
+    for c in range(SEP_CHUNKS):
+        forward(c)
+    for c in range(SEP_CHUNKS):
+        near_copy(c).wait_recv()
+    joined_separator(own, other, g)
+
+    def after(step):
+        for c in FORWARD[step]:
+            forward(c)
+
+    factor_front(g, m, l_ref, after)
     inverse[...] = g[:, NS:NB]
+    for c in range(len(CHUNKS)):
+        far_copy(c).wait_send()
+        near_copy(c).wait_send()
+        if c >= SEP_CHUNKS:
+            near_copy(c).wait_recv()
+    received[...] = other[...]
+
+
+def quad_factor_stage(pieces):
+    half_gx, half_gy = lax.axis_size("gx") // 2, lax.axis_size("gy") // 2
+    copies = pltpu.SemaphoreType.DMA((len(CHUNKS),))
+    return pl.pallas_call(
+        functools.partial(quad_factor_kernel, half_gx, half_gy),
+        out_shape=(SQUARE, SQUARE, PIECES),
+        in_specs=[VMEM],
+        out_specs=(VMEM,) * 3,
+        scratch_shapes=[
+            pltpu.VMEM((BLOCKS, B, B), F32),
+            pltpu.VMEM((NS, NB), F32),
+            pltpu.VMEM((B, 2 * B), F32),
+            copies,
+            copies,
+            copies,
+            copies,
+        ],
+        compiler_params=pltpu.CompilerParams(collective_id=0, has_side_effects=True, vmem_limit_bytes=24 * 2**20),
+        cost_estimate=pl.CostEstimate(flops=10**10, bytes_accessed=4 * 10**6, transcendentals=0),
+        name="quad_factor",
+    )(pieces)
 
 
 def factor_stage(own, other):
@@ -325,20 +408,20 @@
     rest_product(v2, rs_setter(rs, lambda a, b, block: block), setter(rr, lambda t, block: block))
 
 
-def pair_update_kernel(pair_ref, quad_ref, ss_in, rs_in, rr_in, rr_own, rr_other, ss, rs, rr, blocks):
+def pair_update_kernel(pair_ref, quad_ref, ss_in, rs_in, rr_in, rr_own, rr_other, out, blocks):
     _, source = pair_order(pair_ref, quad_ref)
     spread_rest(rr_own, rr_other, blocks)
     for t, (a, b) in enumerate(LOWER):
-        ss[t] = blocks[block_at(source, a, b)] - ss_in[t]
-        rr[t] = blocks[block_at(source, 4 + a, 4 + b)] - rr_in[t]
+        out[t] = blocks[block_at(source, a, b)] - ss_in[t]
+        out[RR0 + t] = blocks[block_at(source, 4 + a, 4 + b)] - rr_in[t]
     for a in range(4):
         for b in range(4):
-            at = (slice(B * a, B * a + B), slice(B * b, B * b + B))
-            rs[at] = blocks[block_at(source, 4 + a, b)] - rs_in[at]
+            out[RS0 + 4 * a + b] = blocks[block_at(source, 4 + a, b)] - rs_in[B * a : B * a + B, B * b : B * b + B]
 
 
 LOWER10 = jax.ShapeDtypeStruct((10, B, B), F32)
 SQUARE = jax.ShapeDtypeStruct((NS, NS), F32)
+PIECES = jax.ShapeDtypeStruct((BLOCKS, B, B), F32)
 PANEL = jax.ShapeDtypeStruct((NJ, NS), F32)
 
 
@@ -357,22 +440,29 @@
         cost_estimate=pl.CostEstimate(flops=3 * 10**9, bytes_accessed=10**7, transcendentals=0),
         name="pair_solve",
     )(pair, quad, l_full, inverse, rs_own, rs_other)
-    ss, rs, rr = pl.pallas_call(
+    pieces = pl.pallas_call(
         pair_update_kernel,
-        out_shape=(LOWER10, SQUARE, LOWER10),
+        out_shape=PIECES,
         in_specs=[SMEM, SMEM] + [VMEM] * 5,
-        out_specs=(VMEM,) * 3,
+        out_specs=VMEM,
         scratch_shapes=[pltpu.VMEM((33, B, B), F32)],
         compiler_params=params(24),
         cost_estimate=pl.CostEstimate(flops=10**6, bytes_accessed=10**7, transcendentals=0),
         name="pair_update",
     )(pair, quad, ss, rs, rr, rr_own, rr_other)
-    return panel, ss, rs, rr
-
-
-def quad_solve_kernel(quad_ref, l_ref, inverse, rs_own, rs_other, panel, lower, bt, vt):
+    return panel, pieces
+
+
+def quad_solve_kernel(quad_ref, l_ref, inverse, own, other, panel, lower, bt, vt):
     source = source_of([quad_ref[0, i] for i in range(8)])
-    gather_rows(rs_own, rs_other, source, bt)
+    for h, pieces in enumerate((own, other)):
+        for a in range(8):
+
+            @pl.when(source[a] // 4 == h)
+            def _(a=a, h=h, pieces=pieces):
+                for b in range(4):
+                    bt[B * a : B * a + B, B * b : B * b + B] = pieces[RS0 + 4 * (source[a] - 4 * h) + b]
+
     panel[0:NS, :] = l_ref[...]
 
     def store(i, rows):
@@ -386,9 +476,9 @@
         lower[rows, 0:last] = dot3((v2[0][rows], v2[1][rows]), (v2[0][0:last], v2[1][0:last]), NT)
 
 
-def quad_update_kernel(quad_ref, lower, rr_own, rr_other, update, blocks):
+def quad_update_kernel(quad_ref, lower, own, other, update, blocks):
     source = source_of([quad_ref[0, i] for i in range(8)])
-    spread_rest(rr_own, rr_other, blocks)
+    spread_rest(own.at[RR0:BLOCKS], other.at[RR0:BLOCKS], blocks)
     for a in range(8):
         for b in range(a + 1):
             block = blocks[block_at(source, a, b)] - lower[B * a : B * a + B, B * b : B * b + B]
@@ -397,7 +487,7 @@
                 update[B * b : B * b + B, B * a : B * a + B] = block.T
 
 
-def quad_stage(quad, l_full, inverse, rs_own, rs_other, rr_own, rr_other):
+def quad_stage(quad, l_full, inverse, own, other):
     panel, lower = pl.pallas_call(
         quad_solve_kernel,
         out_shape=(PANEL, jax.ShapeDtypeStruct((NB, NB), F32)),
@@ -407,7 +497,7 @@
         compiler_params=params(32),
         cost_estimate=pl.CostEstimate(flops=4 * 10**9, bytes_accessed=10**7, transcendentals=0),
         name="quad_solve",
-    )(quad, l_full, inverse, rs_own, rs_other)
+    )(quad, l_full, inverse, own, other)
     update = pl.pallas_call(
         quad_update_kernel,
         out_shape=jax.ShapeDtypeStruct((NB, NB), F32),
@@ -417,7 +507,7 @@
         compiler_params=params(24),
         cost_estimate=pl.CostEstimate(flops=10**6, bytes_accessed=10**7, transcendentals=0),
         name="quad_update",
-    )(quad, lower, rr_own, rr_other)
+    )(quad, lower, own, other)
     return panel, update
 
 
@@ -432,10 +522,9 @@
     rs, rr = rest()
     other_rs, other_rr = swapped(rs, "gx"), swapped(rr, "gx")
     l_pair, inverse = factor_stage(ss, other_ss)
-    pair_panel, ss, rs, rr = pair_stage(place_pairs, place_quads, l_pair, inverse, rs, other_rs, rr, other_rr)
-    other_ss, other_rs, other_rr = swapped(ss, "gy"), swapped(rs, "gy"), swapped(rr, "gy")
-    l_quad, inverse = factor_stage(ss, other_ss)
-    quad_panel, quad_update = quad_stage(place_quads, l_quad, inverse, rs, other_rs, rr, other_rr)
+    pair_panel, pieces = pair_stage(place_pairs, place_quads, l_pair, inverse, rs, other_rs, rr, other_rr)
+    l_quad, inverse, other = quad_factor_stage(pieces)
+    quad_panel, quad_update = quad_stage(place_quads, l_quad, inverse, pieces, other)
     return pair_panel, quad_panel, quad_update
 
 

time: 140 us -> 134 us (0.957)
  Pallas kernels: 86.7 us -> 109 us
  waiting for transfers between devices: 37.8 us -> 15.8 us
  starting transfers between devices: 14.3 us -> 7.66 us
    pallas_call x1 -> x2, Pallas kernels: 1.34 us -> 42.6 us  [the longest x1 41.3 us: quad_factor_stage(): pl.pallas_call(functools.partial(quad_factor_kernel, half_gx, half_gy), o...]
    ppermute x6 -> x3, waiting for transfers between devices: 37.8 us -> 15.8 us  [swapped(): lax.ppermute(value, axis, [(i, (i + size // 2) % size) for i in range(siz...]
    pallas_call x2 -> x1, Pallas kernels: 38.2 us -> 19.1 us  [factor_stage(): pl.pallas_call(factor_kernel, out_shape=(jax.ShapeDtypeStruct((NS, NS), F...]
    ppermute x6 -> x3, starting transfers between devices: 14.3 us -> 7.66 us  [swapped(): lax.ppermute(value, axis, [(i, (i + size // 2) % size) for i in range(siz...]
  transfers between devices with their start and end apart: 6 -> 3, of which waited for: 6 -> 3; matrix products, arithmetic and copies ran while one was open for 0% -> 0% of each run, Pallas kernels for 41% -> 24%
where the time goes in v3:
time: 134 us
  Pallas kernels  109 us (81%)
  waiting for transfers between devices  15.8 us (12%)
  starting transfers between devices  7.66 us (6%)
    pallas_call x1, Pallas kernels, quad_factor_stage(): pl.pallas_call(functools.partial(quad_factor_kernel, half_gx, half_gy), o...  41.3 us
    pallas_call x1, Pallas kernels, leaf_stage(): pl.pallas_call(leaf_solve_kernel, out_shape=(jax.ShapeDtypeStruct((NB, NS...  24.4 us
    pallas_call x1, Pallas kernels, factor_stage(): pl.pallas_call(factor_kernel, out_shape=(jax.ShapeDtypeStruct((NS, NS), F...  19.1 us
    ppermute x3, waiting for transfers between devices, swapped(): lax.ppermute(value, axis, [(i, (i + size // 2) % size) for i in range(siz...  15.8 us
    ppermute x3, starting transfers between devices, swapped(): lax.ppermute(value, axis, [(i, (i + size // 2) % size) for i in range(siz...  7.66 us
    pallas_call x1, Pallas kernels, pair_stage(): pl.pallas_call(pair_solve_kernel, out_shape=(PANEL, LOWER10, SQUARE, LOWE...  6.79 us
    pallas_call x1, Pallas kernels, quad_stage(): pl.pallas_call(quad_solve_kernel, out_shape=(PANEL, jax.ShapeDtypeStruct(...  6.73 us
    pallas_call x1, Pallas kernels, rest(): pl.pallas_call(leaf_rest_kernel, out_shape=(jax.ShapeDtypeStruct((NS, NS)...  6.13 us
  transfers between devices with their start and end apart: 3, of which 3 were waited for; matrix products, arithmetic and copies ran while one was open for 0% of the time, Pallas kernels for 24%

profile of v3, /device:TPU:0, one launch (start us, length us, event | category | flops | bytes accessed | tf_op | source)
XLA Modules:
  0.0 133.5 jit_solution(3822006946715372755)
XLA Ops:
  0.6 24.4 %leaf_solve.1 = (f32[1024,512]{1,0:T(8,128)}, f32[10,128,128]{2,1,0:T(8,128)}) custom-call(s32[1,8]{1,0:T(1,128)} %pair_ref.3, f32[1536,1536]{1,0:T(8,128)} %leaf.3), custom_call_target="tpu_custom_call" | custom-call | flops 10000000000 | bytes 10000000 | tf_op jit(solution)/shard_map/leaf_solve/pallas_call | solution.py:229
  25.1 4.1 %collective-permute-start = (f32[10,128,128]{2,1,0:T(8,128)}, f32[10,128,128]{2,1,0:T(8,128)S(1)}, u32[]{:S(2)}, u32[]{:S(2)}) collective-permute-start(f32[10,128,128]{2,1,0:T(8,128)} %get-tuple-element.18.own), channel_id=1, source_target_pairs={{0,64},{16,80},{32,96},{48,112},{64,0},{80,16},{96,32},{112,48},{1... | collective-permute-start | bytes 1966088 | tf_op jit(solution)/shard_map/ppermute | solution.py:516
  29.1 0.0 copy-start.4
  29.1 6.1 %leaf_rest.1 = (f32[512,512]{1,0:T(8,128)}, f32[10,128,128]{2,1,0:T(8,128)}) custom-call(s32[1,8]{1,0:T(1,128)} %pair_ref.3, f32[1536,1536]{1,0:T(8,128)} %leaf.3, f32[1024,512]{1,0:T(8,128)} %get-tuple-element.21.vt), custom_call_target="tpu_custom_call" | custom-call | flops 3000000000 | bytes 10000000 | tf_op jit(solution)/shard_map/leaf_rest/pallas_call | solution.py:248
  35.3 0.1 collective-permute-start.1
  35.4 0.0 copy-start.1
  35.4 0.0 copy-start.2
  35.4 0.0 copy-start.3
  35.4 3.5 %collective-permute-start.2 = (f32[10,128,128]{2,1,0:T(8,128)}, f32[10,128,128]{2,1,0:T(8,128)S(1)}, u32[]{:S(2)}, u32[]{:S(2)}) collective-permute-start(f32[10,128,128]{2,1,0:T(8,128)} %get-tuple-element.27.rr_own), channel_id=1, source_target_pairs={{0,64},{16,80},{32,96},{48,112},{64,0},{80,16},{96,32},{112,48},{1... | collective-permute-start | bytes 1966088 | tf_op jit(solution)/shard_map/ppermute | solution.py:516
  38.9 6.0 %collective-permute-done.other = f32[10,128,128]{2,1,0:T(8,128)S(1)} collective-permute-done((f32[10,128,128]{2,1,0:T(8,128)}, f32[10,128,128]{2,1,0:T(8,128)S(1)}, u32[]{:S(2)}, u32[]{:S(2)}) %collective-permute-start) | collective-permute-done | bytes 655392 | tf_op jit(solution)/shard_map/ppermute | solution.py:516
  44.9 0.0 copy-done.4
  44.9 19.1 %factor.1 = (f32[512,512]{1,0:T(8,128)S(1)}, f32[512,512]{1,0:T(8,128)S(1)}) custom-call(f32[10,128,128]{2,1,0:T(8,128)S(1)} %copy-done.4, f32[10,128,128]{2,1,0:T(8,128)S(1)} %collective-permute-done.other), custom_call_target="tpu_custom_call" | custom-call | flops 10000000000 | bytes 4000000 | tf_op jit(solution)/shard_map/factor/pallas_call | solution.py:351
  64.0 3.3 %collective-permute-done.1.rs_other = f32[512,512]{1,0:T(8,128)S(1)} collective-permute-done((f32[512,512]{1,0:T(8,128)}, f32[512,512]{1,0:T(8,128)S(1)}, u32[]{:S(2)}, u32[]{:S(2)}) %collective-permute-start.1) | collective-permute-done | bytes 1048608 | tf_op jit(solution)/shard_map/ppermute | solution.py:516
  67.4 0.0 copy-done.1
  67.4 0.0 copy-done.2
  67.4 0.0 copy-done.3
  67.4 0.0 copy-start
  67.4 6.8 %pair_solve.1 = (f32[1536,512]{1,0:T(8,128)}, f32[10,128,128]{2,1,0:T(8,128)S(1)}, f32[512,512]{1,0:T(8,128)S(1)}, f32[10,128,128]{2,1,0:T(8,128)S(1)}) custom-call(s32[1,8]{1,0:T(1,128)S(1)} %copy-done.1, s32[1,8]{1,0:T(1,128)S(1)} %copy-done.2, f32[512,512]{1,0:T(8,128)S(1)} %get-tuple-element.19.l_ref, f32[512,512]{1,0:T(8,128)S(1)} %get-tuple-element.20.inverse, ...), custom_call_target="tpu_custom_call" | custom-call | flops 3000000000 | bytes 10000000 | tf_op jit(solution)/shard_map/pair_solve/pallas_call | solution.py:433
  74.2 6.4 %collective-permute-done.2.rr_other = f32[10,128,128]{2,1,0:T(8,128)S(1)} collective-permute-done((f32[10,128,128]{2,1,0:T(8,128)}, f32[10,128,128]{2,1,0:T(8,128)S(1)}, u32[]{:S(2)}, u32[]{:S(2)}) %collective-permute-start.2) | collective-permute-done | bytes 655392 | tf_op jit(solution)/shard_map/ppermute | solution.py:516
  80.6 0.0 copy-done
  80.6 1.3 pair_update.1.own
  81.9 41.3 %quad_factor.1 = (f32[512,512]{1,0:T(8,128)S(1)}, f32[512,512]{1,0:T(8,128)S(1)}, f32[36,128,128]{2,1,0:T(8,128)S(1)}) custom-call(f32[36,128,128]{2,1,0:T(8,128)S(1)} %pair_update.1.own), custom_call_target="tpu_custom_call" | custom-call | flops 10000000000 | bytes 4000000 | tf_op jit(solution)/shard_map/quad_factor/pallas_call | solution.py:330
  123.2 6.7 %quad_solve.1 = (f32[1536,512]{1,0:T(8,128)}, f32[1024,1024]{1,0:T(8,128)S(1)}) custom-call(s32[1,8]{1,0:T(1,128)S(1)} %copy-done.2, f32[512,512]{1,0:T(8,128)S(1)} %get-tuple-element.28.l_ref, f32[512,512]{1,0:T(8,128)S(1)} %get-tuple-element.29.inverse, f32[36,128,128]{2,1,0:T(8,128)S(1)} %pair_update.1.own, f32[36,128,128]{2,1,0:T(8,128)S(1)} %get-tuple-element.30.other), custom_call_target="tpu_custom_call" | custom-call | flops 4000000000 | bytes 10000000 | tf_op jit(solution)/shard_map/quad_solve/pallas_call | solution.py:491
  130.0 3.6 %quad_update.1 = f32[1024,1024]{1,0:T(8,128)} custom-call(s32[1,8]{1,0:T(1,128)S(1)} %copy-done.2, f32[1024,1024]{1,0:T(8,128)S(1)} %get-tuple-element.32.lower, f32[36,128,128]{2,1,0:T(8,128)S(1)} %pair_update.1.own, f32[36,128,128]{2,1,0:T(8,128)S(1)} %get-tuple-element.30.other), custom_call_target="tpu_custom_call" | custom-call | flops 1000000 | bytes 10000000 | tf_op jit(solution)/shard_map/quad_update/pallas_call | solution.py:501
Async XLA Ops:
  25.1 19.9 %collective-permute-start = (f32[10,128,128]{2,1,0:T(8,128)}, f32[10,128,128]{2,1,0:T(8,128)S(1)}, u32[]{:S(2)}, u32[]{:S(2)}) collective-permute-start(f32[10,128,128]{2,1,0:T(8,128)} %get-tuple-element.18.own), channel_id=1, source_target_pairs={{0,64},{16,80},{32,96},{48,112},{64,0},{80,16},{96,32},{112,48},{1... | collective-permute-start | bytes 1966088 | tf_op jit(solution)/shard_map/ppermute | solution.py:516
  29.1 15.8 %copy-start.4 = (f32[10,128,128]{2,1,0:T(8,128)S(1)}, f32[10,128,128]{2,1,0:T(8,128)}, u32[]{:S(2)}) copy-start(f32[10,128,128]{2,1,0:T(8,128)} %get-tuple-element.18.own) | copy-start | bytes 1966084
  35.3 32.1 %collective-permute-start.1 = (f32[512,512]{1,0:T(8,128)}, f32[512,512]{1,0:T(8,128)S(1)}, u32[]{:S(2)}, u32[]{:S(2)}) collective-permute-start(f32[512,512]{1,0:T(8,128)} %get-tuple-element.22.rs_own), channel_id=1, source_target_pairs={{0,64},{16,80},{32,96},{48,112},{64,0},{80,16},{96,32},{112,48},{1... | collective-permute-start | bytes 3145736 | tf_op jit(solution)/shard_map/ppermute | solution.py:516
  35.4 32.0 %copy-start.1 = (s32[1,8]{1,0:T(1,128)S(1)}, s32[1,8]{1,0:T(1,128)}, u32[]{:S(2)}) copy-start(s32[1,8]{1,0:T(1,128)} %pair_ref.3) | copy-start | bytes 100
  35.4 32.0 %copy-start.2 = (s32[1,8]{1,0:T(1,128)S(1)}, s32[1,8]{1,0:T(1,128)}, u32[]{:S(2)}) copy-start(s32[1,8]{1,0:T(1,128)} %quad_ref.7) | copy-start | bytes 100
  35.4 32.0 %copy-start.3 = (f32[512,512]{1,0:T(8,128)S(1)}, f32[512,512]{1,0:T(8,128)}, u32[]{:S(2)}) copy-start(f32[512,512]{1,0:T(8,128)} %get-tuple-element.22.rs_own) | copy-start | bytes 3145732
  35.4 45.2 %collective-permute-start.2 = (f32[10,128,128]{2,1,0:T(8,128)}, f32[10,128,128]{2,1,0:T(8,128)S(1)}, u32[]{:S(2)}, u32[]{:S(2)}) collective-permute-start(f32[10,128,128]{2,1,0:T(8,128)} %get-tuple-element.27.rr_own), channel_id=1, source_target_pairs={{0,64},{16,80},{32,96},{48,112},{64,0},{80,16},{96,32},{112,48},{1... | collective-permute-start | bytes 1966088 | tf_op jit(solution)/shard_map/ppermute | solution.py:516
  67.4 13.2 %copy-start = (f32[10,128,128]{2,1,0:T(8,128)S(1)}, f32[10,128,128]{2,1,0:T(8,128)}, u32[]{:S(2)}) copy-start(f32[10,128,128]{2,1,0:T(8,128)} %get-tuple-element.27.rr_own) | copy-start | bytes 1966084

commit v4 on v3

--- a/solution.py
+++ b/solution.py
@@ -44,40 +44,48 @@
 NT = ((1,), (1,))
 
 
+def factor_columns(m, p, last):
+    r = 8 * p
+    xs = [full(m[r + i : r + i + 1, 0:B]) for i in range(8)]
+    ys = [full(m[r + i : r + i + 1, B : 2 * B]) for i in range(8)]
+    e = [[full(xs[i][:, r + j : r + j + 1]) if j >= i else None for j in range(8)] for i in range(8)]
+    inv = [None] * 8
+    for k in range(8):
+        inv[k] = lax.rsqrt(e[k][k])
+        for j in range(k + 1, 8):
+            e[k][j] = e[k][j] * inv[k]
+        xs[k], ys[k] = xs[k] * inv[k], ys[k] * inv[k]
+        for i in range(k + 1, 8):
+            for j in range(i, 8):
+                e[i][j] = e[i][j] - e[k][i] * e[k][j]
+            xs[i] = xs[i] - e[k][i] * xs[k]
+            ys[i] = ys[i] - e[k][i] * ys[k]
+    for k in range(8):
+        m[r + k : r + k + 1, 0:B] = xs[k][0:1, :]
+        m[r + k : r + k + 1, B : 2 * B] = ys[k][0:1, :]
+    for q in range(p + 1, last):
+        t = 8 * q
+        y0, y1 = m[t : t + 8, 0:B], m[t : t + 8, B : 2 * B]
+        c = [full(y0[:, r + j : r + j + 1]) for j in range(8)]
+        for k in range(8):
+            c[k] = c[k] * inv[k]
+            for j in range(k + 1, 8):
+                c[j] = c[j] - c[k] * e[k][j]
+            y0 = y0 - c[k] * xs[k]
+            y1 = y1 - c[k] * ys[k]
+        m[t : t + 8, 0:B] = y0
+        m[t : t + 8, B : 2 * B] = y1
+
+
 def factor_block(m):
-    for p in range(B // 8):
-        r = 8 * p
-        x0, x1 = m[r : r + 8, 0:B], m[r : r + 8, B : 2 * B]
-        xs = [full(x0[i : i + 1, :]) for i in range(8)]
-        ys = [full(x1[i : i + 1, :]) for i in range(8)]
-        col = [full(x0[:, r + j : r + j + 1]) for j in range(8)]
-        e = [[full(col[j][i : i + 1, :]) if j >= i else None for j in range(8)] for i in range(8)]
-        inv = [None] * 8
-        for k in range(8):
-            inv[k] = lax.rsqrt(e[k][k])
-            for j in range(k + 1, 8):
-                e[k][j] = e[k][j] * inv[k]
-            xs[k], ys[k] = xs[k] * inv[k], ys[k] * inv[k]
-            for i in range(k + 1, 8):
-                for j in range(i, 8):
-                    e[i][j] = e[i][j] - e[k][i] * e[k][j]
-                xs[i] = xs[i] - e[k][i] * xs[k]
-                ys[i] = ys[i] - e[k][i] * ys[k]
-        for k in range(8):
-            m[r + k : r + k + 1, 0:B] = xs[k][0:1, :]
-            m[r + k : r + k + 1, B : 2 * B] = ys[k][0:1, :]
-        for q in range(p + 1, B // 8):
-            s = 8 * q
-            y0, y1 = m[s : s + 8, 0:B], m[s : s + 8, B : 2 * B]
-            c = [full(y0[:, r + j : r + j + 1]) for j in range(8)]
-            for k in range(8):
-                c[k] = c[k] * inv[k]
-                for j in range(k + 1, 8):
-                    c[j] = c[j] - c[k] * e[k][j]
-                y0 = y0 - c[k] * xs[k]
-                y1 = y1 - c[k] * ys[k]
-            m[s : s + 8, 0:B] = y0
-            m[s : s + 8, B : 2 * B] = y1
+    half = B // 2
+    for p in range(half // 8):
+        factor_columns(m, p, half // 8)
+    top = m[0:half, :]
+    below = top[:, 0:B].T
+    m[half:B, :] = m[half:B, :] - dot3(split(below[half:B, :]), split(top), NN)
+    for p in range(half // 8, B // 8):
+        factor_columns(m, p, B // 8)
 
 
 def eye_block():
@@ -453,7 +461,7 @@
     return panel, pieces
 
 
-def quad_solve_kernel(quad_ref, l_ref, inverse, own, other, panel, lower, bt, vt):
+def quad_kernel(quad_ref, l_ref, inverse, own, other, panel, update, bt, vt, blocks):
     source = source_of([quad_ref[0, i] for i in range(8)])
     for h, pieces in enumerate((own, other)):
         for a in range(8):
@@ -469,46 +477,32 @@
         panel[NS + B * i : NS + B * i + B, :] = rows
 
     solve_rows(bt, inverse[...], vt, store)
+    spread_rest(own.at[RR0:BLOCKS], other.at[RR0:BLOCKS], blocks)
     v2 = split(vt[...])
     for h in range(4):
         rows = slice(256 * h, 256 * (h + 1))
         last = 256 * (h + 1)
-        lower[rows, 0:last] = dot3((v2[0][rows], v2[1][rows]), (v2[0][0:last], v2[1][0:last]), NT)
-
-
-def quad_update_kernel(quad_ref, lower, own, other, update, blocks):
-    source = source_of([quad_ref[0, i] for i in range(8)])
-    spread_rest(own.at[RR0:BLOCKS], other.at[RR0:BLOCKS], blocks)
-    for a in range(8):
-        for b in range(a + 1):
-            block = blocks[block_at(source, a, b)] - lower[B * a : B * a + B, B * b : B * b + B]
-            update[B * a : B * a + B, B * b : B * b + B] = block
-            if a != b:
-                update[B * b : B * b + B, B * a : B * a + B] = block.T
+        prod = dot3((v2[0][rows], v2[1][rows]), (v2[0][0:last], v2[1][0:last]), NT)
+        for a in (2 * h, 2 * h + 1):
+            r = B * (a % 2)
+            for b in range(a + 1):
+                block = blocks[block_at(source, a, b)] - prod[r : r + B, B * b : B * b + B]
+                update[B * a : B * a + B, B * b : B * b + B] = block
+                if a != b:
+                    update[B * b : B * b + B, B * a : B * a + B] = block.T
 
 
 def quad_stage(quad, l_full, inverse, own, other):
-    panel, lower = pl.pallas_call(
-        quad_solve_kernel,
+    return pl.pallas_call(
+        quad_kernel,
         out_shape=(PANEL, jax.ShapeDtypeStruct((NB, NB), F32)),
         in_specs=[SMEM] + [VMEM] * 4,
         out_specs=(VMEM, VMEM),
-        scratch_shapes=[pltpu.VMEM((NB, NS), F32), pltpu.VMEM((NB, NS), F32)],
+        scratch_shapes=[pltpu.VMEM((NB, NS), F32), pltpu.VMEM((NB, NS), F32), pltpu.VMEM((33, B, B), F32)],
         compiler_params=params(32),
         cost_estimate=pl.CostEstimate(flops=4 * 10**9, bytes_accessed=10**7, transcendentals=0),
-        name="quad_solve",
+        name="quad",
     )(quad, l_full, inverse, own, other)
-    update = pl.pallas_call(
-        quad_update_kernel,
-        out_shape=jax.ShapeDtypeStruct((NB, NB), F32),
-        in_specs=[SMEM] + [VMEM] * 3,
-        out_specs=VMEM,
-        scratch_shapes=[pltpu.VMEM((33, B, B), F32)],
-        compiler_params=params(24),
-        cost_estimate=pl.CostEstimate(flops=10**6, bytes_accessed=10**7, transcendentals=0),
-        name="quad_update",
-    )(quad, lower, own, other)
-    return panel, update
 
 
 def swapped(value, axis):

time: 134 us -> 124 us (0.925)
  Pallas kernels: 109 us -> 94.6 us
  waiting for transfers between devices: 15.8 us -> 21.3 us
    ppermute x3, waiting for transfers between devices: 15.8 us -> 21.3 us  [swapped(): lax.ppermute(value, axis, [(i, (i + size // 2) % size) for i in range(siz...]
    pallas_call x1, Pallas kernels: 19.1 us -> 13.8 us  [factor_stage(): pl.pallas_call(factor_kernel, out_shape=(jax.ShapeDtypeStruct((NS, NS), F...]
    pallas_call x1, Pallas kernels: 24.4 us -> 19.1 us  [leaf_stage(): pl.pallas_call(leaf_solve_kernel, out_shape=(jax.ShapeDtypeStruct((NB, NS...]
    pallas_call x2 -> x1, Pallas kernels: 10.3 us -> 8.19 us  [quad_stage(): pl.pallas_call(quad_kernel, out_shape=(PANEL, jax.ShapeDtypeStruct((NB, N...]
    pallas_call x1, Pallas kernels: 41.3 us -> 39.4 us  [quad_factor_stage(): pl.pallas_call(functools.partial(quad_factor_kernel, half_gx, half_gy), o...]
  transfers between devices with their start and end apart: 3 -> 3, of which waited for: 3 -> 3; matrix products, arithmetic and copies ran while one was open for 0% -> 0% of each run, Pallas kernels for 24% -> 21%
where the time goes in v4:
time: 124 us
  Pallas kernels  94.6 us (76%)
  waiting for transfers between devices  21.3 us (17%)
  starting transfers between devices  7.66 us (6%)
    pallas_call x1, Pallas kernels, quad_factor_stage(): pl.pallas_call(functools.partial(quad_factor_kernel, half_gx, half_gy), o...  39.4 us
    ppermute x3, waiting for transfers between devices, swapped(): lax.ppermute(value, axis, [(i, (i + size // 2) % size) for i in range(siz...  21.3 us
    pallas_call x1, Pallas kernels, leaf_stage(): pl.pallas_call(leaf_solve_kernel, out_shape=(jax.ShapeDtypeStruct((NB, NS...  19.1 us
    pallas_call x1, Pallas kernels, factor_stage(): pl.pallas_call(factor_kernel, out_shape=(jax.ShapeDtypeStruct((NS, NS), F...  13.8 us
    pallas_call x1, Pallas kernels, quad_stage(): pl.pallas_call(quad_kernel, out_shape=(PANEL, jax.ShapeDtypeStruct((NB, N...  8.19 us
    ppermute x3, starting transfers between devices, swapped(): lax.ppermute(value, axis, [(i, (i + size // 2) % size) for i in range(siz...  7.66 us
    pallas_call x1, Pallas kernels, pair_stage(): pl.pallas_call(pair_solve_kernel, out_shape=(PANEL, LOWER10, SQUARE, LOWE...  6.57 us
    pallas_call x1, Pallas kernels, rest(): pl.pallas_call(leaf_rest_kernel, out_shape=(jax.ShapeDtypeStruct((NS, NS)...  6.13 us
  transfers between devices with their start and end apart: 3, of which 3 were waited for; matrix products, arithmetic and copies ran while one was open for 0% of the time, Pallas kernels for 21%

profile of v4, /device:TPU:0, one launch (start us, length us, event | category | flops | bytes accessed | tf_op | source)
XLA Modules:
  0.0 124.2 jit_solution(9699725870105167195)
XLA Ops:
  0.6 19.1 %leaf_solve.1 = (f32[1024,512]{1,0:T(8,128)}, f32[10,128,128]{2,1,0:T(8,128)}) custom-call(s32[1,8]{1,0:T(1,128)} %pair_ref.3, f32[1536,1536]{1,0:T(8,128)} %leaf.3), custom_call_target="tpu_custom_call" | custom-call | flops 10000000000 | bytes 10000000 | tf_op jit(solution)/shard_map/leaf_solve/pallas_call | solution.py:237
  19.8 4.1 %collective-permute-start = (f32[10,128,128]{2,1,0:T(8,128)}, f32[10,128,128]{2,1,0:T(8,128)S(1)}, u32[]{:S(2)}, u32[]{:S(2)}) collective-permute-start(f32[10,128,128]{2,1,0:T(8,128)} %get-tuple-element.18.own), channel_id=1, source_target_pairs={{0,64},{16,80},{32,96},{48,112},{64,0},{80,16},{96,32},{112,48},{1... | collective-permute-start | bytes 1966088 | tf_op jit(solution)/shard_map/ppermute | solution.py:510
  23.8 0.0 copy-start.4
  23.8 6.1 %leaf_rest.1 = (f32[512,512]{1,0:T(8,128)}, f32[10,128,128]{2,1,0:T(8,128)}) custom-call(s32[1,8]{1,0:T(1,128)} %pair_ref.3, f32[1536,1536]{1,0:T(8,128)} %leaf.3, f32[1024,512]{1,0:T(8,128)} %get-tuple-element.21.vt), custom_call_target="tpu_custom_call" | custom-call | flops 3000000000 | bytes 10000000 | tf_op jit(solution)/shard_map/leaf_rest/pallas_call | solution.py:256
  30.0 0.1 collective-permute-start.1
  30.1 0.0 copy-start.1
  30.1 0.0 copy-start.2
  30.1 0.0 copy-start.3
  30.1 3.5 %collective-permute-start.2 = (f32[10,128,128]{2,1,0:T(8,128)}, f32[10,128,128]{2,1,0:T(8,128)S(1)}, u32[]{:S(2)}, u32[]{:S(2)}) collective-permute-start(f32[10,128,128]{2,1,0:T(8,128)} %get-tuple-element.27.rr_own), channel_id=1, source_target_pairs={{0,64},{16,80},{32,96},{48,112},{64,0},{80,16},{96,32},{112,48},{1... | collective-permute-start | bytes 1966088 | tf_op jit(solution)/shard_map/ppermute | solution.py:510
  33.6 6.0 %collective-permute-done.other = f32[10,128,128]{2,1,0:T(8,128)S(1)} collective-permute-done((f32[10,128,128]{2,1,0:T(8,128)}, f32[10,128,128]{2,1,0:T(8,128)S(1)}, u32[]{:S(2)}, u32[]{:S(2)}) %collective-permute-start) | collective-permute-done | bytes 655392 | tf_op jit(solution)/shard_map/ppermute | solution.py:510
  39.6 0.0 copy-done.4
  39.6 13.8 %factor.1 = (f32[512,512]{1,0:T(8,128)S(1)}, f32[512,512]{1,0:T(8,128)S(1)}) custom-call(f32[10,128,128]{2,1,0:T(8,128)S(1)} %copy-done.4, f32[10,128,128]{2,1,0:T(8,128)S(1)} %collective-permute-done.other), custom_call_target="tpu_custom_call" | custom-call | flops 10000000000 | bytes 4000000 | tf_op jit(solution)/shard_map/factor/pallas_call | solution.py:359
  53.4 8.7 %collective-permute-done.1.rs_other = f32[512,512]{1,0:T(8,128)S(1)} collective-permute-done((f32[512,512]{1,0:T(8,128)}, f32[512,512]{1,0:T(8,128)S(1)}, u32[]{:S(2)}, u32[]{:S(2)}) %collective-permute-start.1) | collective-permute-done | bytes 1048608 | tf_op jit(solution)/shard_map/ppermute | solution.py:510
  62.1 0.0 copy-done.1
  62.1 0.0 copy-done.2
  62.1 0.0 copy-done.3
  62.1 0.0 copy-start
  62.1 6.6 %pair_solve.1 = (f32[1536,512]{1,0:T(8,128)}, f32[10,128,128]{2,1,0:T(8,128)S(1)}, f32[512,512]{1,0:T(8,128)S(1)}, f32[10,128,128]{2,1,0:T(8,128)S(1)}) custom-call(s32[1,8]{1,0:T(1,128)S(1)} %copy-done.1, s32[1,8]{1,0:T(1,128)S(1)} %copy-done.2, f32[512,512]{1,0:T(8,128)S(1)} %get-tuple-element.19.l_ref, f32[512,512]{1,0:T(8,128)S(1)} %get-tuple-element.20.inverse, ...), custom_call_target="tpu_custom_call" | custom-call | flops 3000000000 | bytes 10000000 | tf_op jit(solution)/shard_map/pair_solve/pallas_call | solution.py:441
  68.7 6.6 %collective-permute-done.2.rr_other = f32[10,128,128]{2,1,0:T(8,128)S(1)} collective-permute-done((f32[10,128,128]{2,1,0:T(8,128)}, f32[10,128,128]{2,1,0:T(8,128)S(1)}, u32[]{:S(2)}, u32[]{:S(2)}) %collective-permute-start.2) | collective-permute-done | bytes 655392 | tf_op jit(solution)/shard_map/ppermute | solution.py:510
  75.3 0.0 copy-done
  75.3 1.3 %pair_update.1.own = f32[36,128,128]{2,1,0:T(8,128)S(1)} custom-call(s32[1,8]{1,0:T(1,128)S(1)} %copy-done.1, s32[1,8]{1,0:T(1,128)S(1)} %copy-done.2, f32[10,128,128]{2,1,0:T(8,128)S(1)} %get-tuple-element.24.ss_in, f32[512,512]{1,0:T(8,128)S(1)} %get-tuple-element.25.rs_in, f32[10,128,128]{2,1,0:T(8,128)S(1)} %get-tuple-element.26.rr_in, ...), custom_call_target="tpu_custom_call" | custom-call | flops 1000000 | bytes 10000000 | tf_op jit(solution)/shard_map/pair_update/pallas_call | solution.py:451
  76.6 39.4 %quad_factor.1 = (f32[512,512]{1,0:T(8,128)S(1)}, f32[512,512]{1,0:T(8,128)S(1)}, f32[36,128,128]{2,1,0:T(8,128)S(1)}) custom-call(f32[36,128,128]{2,1,0:T(8,128)S(1)} %pair_update.1.own), custom_call_target="tpu_custom_call" | custom-call | flops 10000000000 | bytes 4000000 | tf_op jit(solution)/shard_map/quad_factor/pallas_call | solution.py:338
  116.0 8.2 %quad.1 = (f32[1536,512]{1,0:T(8,128)}, f32[1024,1024]{1,0:T(8,128)}) custom-call(s32[1,8]{1,0:T(1,128)S(1)} %copy-done.2, f32[512,512]{1,0:T(8,128)S(1)} %get-tuple-element.28.l_ref, f32[512,512]{1,0:T(8,128)S(1)} %get-tuple-element.29.inverse, f32[36,128,128]{2,1,0:T(8,128)S(1)} %pair_update.1.own, f32[36,128,128]{2,1,0:T(8,128)S(1)} %get-tuple-element.30.other), custom_call_target="tpu_custom_call" | custom-call | flops 4000000000 | bytes 10000000 | tf_op jit(solution)/shard_map/quad/pallas_call | solution.py:496
Async XLA Ops:
  19.8 19.9 %collective-permute-start = (f32[10,128,128]{2,1,0:T(8,128)}, f32[10,128,128]{2,1,0:T(8,128)S(1)}, u32[]{:S(2)}, u32[]{:S(2)}) collective-permute-start(f32[10,128,128]{2,1,0:T(8,128)} %get-tuple-element.18.own), channel_id=1, source_target_pairs={{0,64},{16,80},{32,96},{48,112},{64,0},{80,16},{96,32},{112,48},{1... | collective-permute-start | bytes 1966088 | tf_op jit(solution)/shard_map/ppermute | solution.py:510
  23.8 15.8 %copy-start.4 = (f32[10,128,128]{2,1,0:T(8,128)S(1)}, f32[10,128,128]{2,1,0:T(8,128)}, u32[]{:S(2)}) copy-start(f32[10,128,128]{2,1,0:T(8,128)} %get-tuple-element.18.own) | copy-start | bytes 1966084
  30.0 32.1 %collective-permute-start.1 = (f32[512,512]{1,0:T(8,128)}, f32[512,512]{1,0:T(8,128)S(1)}, u32[]{:S(2)}, u32[]{:S(2)}) collective-permute-start(f32[512,512]{1,0:T(8,128)} %get-tuple-element.22.rs_own), channel_id=1, source_target_pairs={{0,64},{16,80},{32,96},{48,112},{64,0},{80,16},{96,32},{112,48},{1... | collective-permute-start | bytes 3145736 | tf_op jit(solution)/shard_map/ppermute | solution.py:510
  30.1 32.0 %copy-start.1 = (s32[1,8]{1,0:T(1,128)S(1)}, s32[1,8]{1,0:T(1,128)}, u32[]{:S(2)}) copy-start(s32[1,8]{1,0:T(1,128)} %pair_ref.3) | copy-start | bytes 100
  30.1 32.0 %copy-start.2 = (s32[1,8]{1,0:T(1,128)S(1)}, s32[1,8]{1,0:T(1,128)}, u32[]{:S(2)}) copy-start(s32[1,8]{1,0:T(1,128)} %quad_ref.5) | copy-start | bytes 100
  30.1 32.0 %copy-start.3 = (f32[512,512]{1,0:T(8,128)S(1)}, f32[512,512]{1,0:T(8,128)}, u32[]{:S(2)}) copy-start(f32[512,512]{1,0:T(8,128)} %get-tuple-element.22.rs_own) | copy-start | bytes 3145732
  30.1 45.2 %collective-permute-start.2 = (f32[10,128,128]{2,1,0:T(8,128)}, f32[10,128,128]{2,1,0:T(8,128)S(1)}, u32[]{:S(2)}, u32[]{:S(2)}) collective-permute-start(f32[10,128,128]{2,1,0:T(8,128)} %get-tuple-element.27.rr_own), channel_id=1, source_target_pairs={{0,64},{16,80},{32,96},{48,112},{64,0},{80,16},{96,32},{112,48},{1... | collective-permute-start | bytes 1966088 | tf_op jit(solution)/shard_map/ppermute | solution.py:510
  62.1 13.2 %copy-start = (f32[10,128,128]{2,1,0:T(8,128)S(1)}, f32[10,128,128]{2,1,0:T(8,128)}, u32[]{:S(2)}) copy-start(f32[10,128,128]{2,1,0:T(8,128)} %get-tuple-element.27.rr_own) | copy-start | bytes 1966084
